TPU v7x, 128 devices: a whole 4x4x4 slice. The times are simulated.
128 devices in a mesh: wind: 8 (over z, y_hi), state: 16 (over x, y_lo, core).
Axes of the slice: x: 4, y: 4 (y_hi: 2, y_lo: 2; y = y_hi * 2 + y_lo), z: 4, core: 2. Of those that a mesh axis runs over, the one named last changes fastest.
Arguments:
- value_next: float32 [128, 16, 256, 256], P('wind', None, 'state'), may hold values from -6 to 6
- density: float32 [128, 16, 256, 256], P('wind', None, 'state'), may hold values from 0.1 to 2
- price: float32 [128, 16], P('wind'), may hold values from -4 to 4
- wind_rate: float32 [128, 16], P('wind'), may hold values from 0.05 to 0.5
- tank_inverse: float32 [256, 256], replicated, may hold values from -0.5 to 1.5
- soc_inverse: float32 [256, 256], replicated, may hold values from -0.5 to 1.5
Outputs:
- value: float32 [128, 16, 256, 256], P('wind', None, 'state')
- density_next: float32 [128, 16, 256, 256], P('wind', None, 'state')
All inputs are finite; a program needn't handle non-finite values.
Results may differ from a plain program's by a relative error of at most 0.0001.
Values sent between devices are 32-bit elements; how exact they have to be, the bound alone decides.
A program may use at most 192 MiB of HBM per device.

v0:
```python
import jax
import jax.numpy as jnp
from jax import lax
from jax.sharding import PartitionSpec as P

ITERS = 4


step_size = 0.25
control_bound = 2.0
control_cost = 1.0
tank_spread = 0.3


def extended(cells, sides, width):
    for axis, dim in sides:
        count = lax.axis_size(axis)
        ends = count - 1
        head = lax.slice_in_dim(cells, 0, width, axis=dim)
        tail = lax.slice_in_dim(cells, cells.shape[dim] - width, cells.shape[dim], axis=dim)
        cells = jnp.concatenate(
            [
                lax.ppermute(tail, axis, [(i, (i + 1) % count) for i in range(ends)]),
                cells,
                lax.ppermute(head, axis, [((i + 1) % count, i) for i in range(ends)]),
            ],
            axis=dim,
        )
    return cells


def control_law(slope, price):
    shifted = slope + price[:, :, None, None]
    action = -control_bound * jnp.tanh(shifted / (control_cost * control_bound))
    hamilton = action * shifted + 0.5 * control_cost * action * action
    return (action, hamilton)


def value_rims(current):
    return extended(current, (("wind", 0), ("state", 2)), 1)


def regroup(block):
    return jnp.swapaxes(block, 2, 3)


def on_device(value_next, density, price, wind_rate, tank_inverse, soc_inverse):
    rates = wind_rate[:, :, None, None]
    current = value_next
    for sweep in range(ITERS):
        padded = value_rims(current)
        slope = 0.5 * (padded[1:-1, :, 2:] - padded[1:-1, :, :-2])
        action, hamilton = control_law(slope, price)
        couple = rates * (padded[2:, :, 1:-1] + padded[:-2, :, 1:-1] - 2.0 * current)
        source = value_next + step_size * (hamilton + couple)
        current = jnp.einsum(
            "wrsk,tk->wrst",
            source,
            tank_inverse,
            precision=lax.Precision.HIGHEST,
            preferred_element_type=jnp.float32,
        )
    padded = extended(current, (("state", 2),), 1)
    slope = 0.5 * (padded[:, :, 2:] - padded[:, :, :-2])
    action, hamilton = control_law(slope, price)
    drift = regroup(lax.all_to_all(action, "state", split_axis=3, concat_axis=2, tiled=True))
    flux_edged = jnp.pad(drift * density, ((0, 0), (0, 0), (0, 0), (1, 1)))
    spread = 0.5 * (flux_edged[:, :, :, 2:] - flux_edged[:, :, :, :-2])
    padded = extended(density, (("wind", 0), ("state", 2)), 1)
    tank_term = tank_spread * (padded[1:-1, :, 2:] + padded[1:-1, :, :-2] - 2.0 * density)
    wind_term = rates * (padded[2:, :, 1:-1] + padded[:-2, :, 1:-1] - 2.0 * density)
    source = density + step_size * (tank_term + wind_term - spread)
    density_next = jnp.einsum(
        "wrks,ts->wrkt",
        source,
        soc_inverse,
        precision=lax.Precision.HIGHEST,
        preferred_element_type=jnp.float32,
    )
    return (current, density_next)


def solution(mesh):
    placed = (
        P("wind", None, "state", None),
        P("wind", None, "state", None),
        P("wind", None),
        P("wind", None),
        P(),
        P(),
    )
    return jax.shard_map(
        on_device,
        mesh=mesh,
        in_specs=placed,
        out_specs=(P("wind", None, "state", None), P("wind", None, "state", None)),
        check_vma=False,
    )
```

profile of v0, /device:TPU:6, one launch (start us, length us, event | category | flops | bytes accessed | tf_op | source)
XLA Modules:
  0.0 408.7 jit_solution(6650672266368128389)
XLA Ops:
  1.8 5.1 %collective-permute-start = (f32[1,16,16,256]{3,2,1,0:T(8,128)S(1)}, f32[1,16,16,256]{3,2,1,0:T(8,128)S(1)}, u32[]{:S(2)}, u32[]{:S(2)}) collective-permute-start(f32[1,16,16,256]{3,2,1,0:T(8,128)S(1)} %get-tuple-element.25), channel_id=1, source_target_pairs={{0,16},{16,32},{32,48},{48,64},{64,80},{80,96},{96,112},{1,17},{17... | collective-permute-start | bytes 786440 | tf_op jit(solution)/shard_map/ppermute | solution.py:23
  8.2 4.2 %collective-permute-done = f32[1,16,16,256]{3,2,1,0:T(8,128)S(1)} collective-permute-done((f32[1,16,16,256]{3,2,1,0:T(8,128)S(1)}, f32[1,16,16,256]{3,2,1,0:T(8,128)S(1)}, u32[]{:S(2)}, u32[]{:S(2)}) %collective-permute-start) | collective-permute-done | bytes 262176 | tf_op jit(solution)/shard_map/ppermute | solution.py:23
  12.5 3.2 constant_dynamic-update-slice_fusion.1
  15.7 4.5 %collective-permute-done.1 = f32[1,16,16,256]{3,2,1,0:T(8,128)S(1)} collective-permute-done((f32[1,16,16,256]{3,2,1,0:T(8,128)S(1)}, f32[1,16,16,256]{3,2,1,0:T(8,128)S(1)}, u32[]{:S(2)}, u32[]{:S(2)}) %collective-permute-start.1) | collective-permute-done | bytes 262176 | tf_op jit(solution)/shard_map/ppermute | solution.py:25
  20.8 2.3 collective-permute-start.2
  23.2 2.0 collective-permute-start.3
  25.2 2.2 collective-permute-done.2
  27.4 4.8 %collective-permute-done.3 = f32[18,16,1,256]{3,2,1,0:T(1,128)S(1)} collective-permute-done((f32[18,16,1,256]{3,2,1,0:T(1,128)S(1)}, f32[18,16,1,256]{3,2,1,0:T(1,128)S(1)}, u32[]{:S(2)}, u32[]{:S(2)}) %collective-permute-start.3) | collective-permute-done | bytes 294944 | tf_op jit(solution)/shard_map/ppermute | solution.py:23
  32.2 7.8 %fusion.72 = f32[16,16,16,256]{3,2,1,0:T(8,128)S(1)} fusion(f32[16,16,16,256]{3,2,1,0:T(8,128)S(1)} %copy-done.3, f32[1,16,16,256]{3,2,1,0:T(8,128)S(1)} %collective-permute-done, f32[1,16,16,256]{3,2,1,0:T(8,128)S(1)} %collective-permute-done.1, f32[18,16,16,256]{3,2,1,0:T(8,128)S(1)} %constant_dynamic-update-slice_fusion, ...), kind=kOutput, calls=%fused_computation.100 | convolution fusion | flops 3241148416 | bytes 14485504 | tf_op jit(solution)/shard_map/wrsk,tk->wrst/dot_general | solution.py:56
  40.0 4.8 %collective-permute-start.4 = (f32[1,16,16,256]{3,2,1,0:T(8,128)S(1)}, f32[1,16,16,256]{3,2,1,0:T(8,128)S(1)}, u32[]{:S(2)}, u32[]{:S(2)}) collective-permute-start(f32[1,16,16,256]{3,2,1,0:T(8,128)S(1)} %get-tuple-element.23), channel_id=1, source_target_pairs={{0,16},{16,32},{32,48},{48,64},{64,80},{80,96},{96,112},{1,17},{17... | collective-permute-start | bytes 786440 | tf_op jit(solution)/shard_map/ppermute | solution.py:23
  46.2 2.6 collective-permute-done.4
  48.7 8.1 %collective-permute-done.5 = f32[1,16,16,256]{3,2,1,0:T(8,128)S(1)} collective-permute-done((f32[1,16,16,256]{3,2,1,0:T(8,128)S(1)}, f32[1,16,16,256]{3,2,1,0:T(8,128)S(1)}, u32[]{:S(2)}, u32[]{:S(2)}) %collective-permute-start.5) | collective-permute-done | bytes 262176 | tf_op jit(solution)/shard_map/ppermute | solution.py:25
  59.3 2.4 collective-permute-start.7
  63.6 4.7 %collective-permute-done.7 = f32[18,16,1,256]{3,2,1,0:T(1,128)S(1)} collective-permute-done((f32[18,16,1,256]{3,2,1,0:T(1,128)S(1)}, f32[18,16,1,256]{3,2,1,0:T(1,128)S(1)}, u32[]{:S(2)}, u32[]{:S(2)}) %collective-permute-start.7) | collective-permute-done | bytes 294944 | tf_op jit(solution)/shard_map/ppermute | solution.py:23
  68.3 8.0 %fusion.59 = f32[16,16,16,256]{3,2,1,0:T(8,128)S(1)} fusion(f32[16,16,16,256]{3,2,1,0:T(8,128)S(1)} %copy-done.3, f32[16,16,16,256]{3,2,1,0:T(8,128)S(1)} %fusion.72, f32[1,16,16,256]{3,2,1,0:T(8,128)S(1)} %collective-permute-done.4, f32[1,16,16,256]{3,2,1,0:T(8,128)S(1)} %collective-permute-done.5, f32[18,16,1,256]{3,2,1,0:T(1,128)S(1)} %collective-permute-done.7, ...), kind=kOutput, calls=%fused_computation.80 | convolution fusion | flops 3245342720 | bytes 13961216 | tf_op jit(solution)/shard_map/wrsk,tk->wrst/dot_general | solution.py:56
  76.4 4.8 %collective-permute-start.8 = (f32[1,16,16,256]{3,2,1,0:T(8,128)S(1)}, f32[1,16,16,256]{3,2,1,0:T(8,128)S(1)}, u32[]{:S(2)}, u32[]{:S(2)}) collective-permute-start(f32[1,16,16,256]{3,2,1,0:T(8,128)S(1)} %get-tuple-element.21), channel_id=1, source_target_pairs={{0,16},{16,32},{32,48},{48,64},{64,80},{80,96},{96,112},{1,17},{17... | collective-permute-start | bytes 786440 | tf_op jit(solution)/shard_map/ppermute | solution.py:23
  82.5 2.6 collective-permute-done.8
  85.1 7.4 %collective-permute-done.9 = f32[1,16,16,256]{3,2,1,0:T(8,128)S(1)} collective-permute-done((f32[1,16,16,256]{3,2,1,0:T(8,128)S(1)}, f32[1,16,16,256]{3,2,1,0:T(8,128)S(1)}, u32[]{:S(2)}, u32[]{:S(2)}) %collective-permute-start.9) | collective-permute-done | bytes 262176 | tf_op jit(solution)/shard_map/ppermute | solution.py:25
  93.1 1.9 collective-permute-start.10
  95.0 2.4 collective-permute-start.11
  99.2 4.7 %collective-permute-done.11 = f32[18,16,1,256]{3,2,1,0:T(1,128)S(1)} collective-permute-done((f32[18,16,1,256]{3,2,1,0:T(1,128)S(1)}, f32[18,16,1,256]{3,2,1,0:T(1,128)S(1)}, u32[]{:S(2)}, u32[]{:S(2)}) %collective-permute-start.11) | collective-permute-done | bytes 294944 | tf_op jit(solution)/shard_map/ppermute | solution.py:23
  104.0 8.0 %fusion.46 = f32[16,16,16,256]{3,2,1,0:T(8,128)S(1)} fusion(f32[16,16,16,256]{3,2,1,0:T(8,128)S(1)} %copy-done.3, f32[16,16,16,256]{3,2,1,0:T(8,128)S(1)} %fusion.59, f32[1,16,16,256]{3,2,1,0:T(8,128)S(1)} %collective-permute-done.8, f32[1,16,16,256]{3,2,1,0:T(8,128)S(1)} %collective-permute-done.9, f32[18,16,1,256]{3,2,1,0:T(1,128)S(1)} %collective-permute-done.11, ...), kind=kOutput, calls=%fused_computation.60 | convolution fusion | flops 3245342720 | bytes 13961216 | tf_op jit(solution)/shard_map/wrsk,tk->wrst/dot_general | solution.py:56
  112.0 4.7 %collective-permute-start.12 = (f32[1,16,16,256]{3,2,1,0:T(8,128)S(1)}, f32[1,16,16,256]{3,2,1,0:T(8,128)S(1)}, u32[]{:S(2)}, u32[]{:S(2)}) collective-permute-start(f32[1,16,16,256]{3,2,1,0:T(8,128)S(1)} %get-tuple-element.19), channel_id=1, source_target_pairs={{0,16},{16,32},{32,48},{48,64},{64,80},{80,96},{96,112},{1,17},{17... | collective-permute-start | bytes 786440 | tf_op jit(solution)/shard_map/ppermute | solution.py:23
  118.0 2.6 collective-permute-done.12
  120.6 7.2 %collective-permute-done.13 = f32[1,16,16,256]{3,2,1,0:T(8,128)S(1)} collective-permute-done((f32[1,16,16,256]{3,2,1,0:T(8,128)S(1)}, f32[1,16,16,256]{3,2,1,0:T(8,128)S(1)}, u32[]{:S(2)}, u32[]{:S(2)}) %collective-permute-start.13) | collective-permute-done | bytes 262176 | tf_op jit(solution)/shard_map/ppermute | solution.py:25
  130.4 2.4 collective-permute-start.15
  134.6 4.7 %collective-permute-done.15 = f32[18,16,1,256]{3,2,1,0:T(1,128)S(1)} collective-permute-done((f32[18,16,1,256]{3,2,1,0:T(1,128)S(1)}, f32[18,16,1,256]{3,2,1,0:T(1,128)S(1)}, u32[]{:S(2)}, u32[]{:S(2)}) %collective-permute-start.15) | collective-permute-done | bytes 294944 | tf_op jit(solution)/shard_map/ppermute | solution.py:23
  139.3 8.0 %fusion.33 = f32[16,16,16,256]{3,2,1,0:T(8,128)S(1)} fusion(f32[16,16,16,256]{3,2,1,0:T(8,128)S(1)} %copy-done.3, f32[16,16,16,256]{3,2,1,0:T(8,128)S(1)} %fusion.46, f32[1,16,16,256]{3,2,1,0:T(8,128)S(1)} %collective-permute-done.12, f32[1,16,16,256]{3,2,1,0:T(8,128)S(1)} %collective-permute-done.13, f32[18,16,1,256]{3,2,1,0:T(1,128)S(1)} %collective-permute-done.15, ...), kind=kOutput, calls=%fused_computation.40 | convolution fusion | flops 3245342720 | bytes 13961216 | tf_op jit(solution)/shard_map/wrsk,tk->wrst/dot_general | solution.py:56
  147.9 1.9 collective-permute-start.20
  149.8 2.4 collective-permute-start.21
  153.7 4.7 %collective-permute-done.21 = f32[16,16,1,256]{3,2,1,0:T(1,128)S(1)} collective-permute-done((f32[16,16,1,256]{3,2,1,0:T(1,128)S(1)}, f32[16,16,1,256]{3,2,1,0:T(1,128)S(1)}, u32[]{:S(2)}, u32[]{:S(2)}) %collective-permute-start.21) | collective-permute-done | bytes 262176 | tf_op jit(solution)/shard_map/ppermute | solution.py:23
  158.4 3.2 fusion.12
  161.7 26.4 %copy.9 = f32[16,16,16,256]{2,1,0,3:T(8,128)} copy(f32[16,16,16,256]{3,2,1,0:T(8,128)} %fusion.12) | data formatting | bytes 8388608 | tf_op jit(solution)/shard_map/mul | solution.py:34
  188.0 22.0 %reshape.8 = f32[16,1,65536]{2,1,0:T(1,128)} reshape(f32[256,16,16,16]{3,2,1,0:T(8,128)} %bitcast.28) | data formatting | bytes 8388608
  210.0 7.1 %all-to-all-start = ((f32[16,1,65536]{2,1,0:T(1,128)}), f32[16,1,65536]{2,1,0:T(1,128)}, u32[]{:S(2)}, u32[]{:S(2)}) async-start(f32[16,1,65536]{2,1,0:T(1,128)} %reshape.8), calls=%async_computation | async-start | bytes 8388608 | tf_op jit(solution)/shard_map/all_to_all | solution.py:66
  218.2 4.3 %collective-permute-start.16 = (f32[1,16,16,256]{3,2,1,0:T(8,128)S(1)}, f32[1,16,16,256]{3,2,1,0:T(8,128)S(1)}, u32[]{:S(2)}, u32[]{:S(2)}) collective-permute-start(f32[1,16,16,256]{3,2,1,0:T(8,128)S(1)} %get-tuple-element.15), channel_id=1, source_target_pairs={{0,16},{16,32},{32,48},{48,64},{64,80},{80,96},{96,112},{1,17},{17... | collective-permute-start | bytes 786440 | tf_op jit(solution)/shard_map/ppermute | solution.py:23
  223.8 44.6 %collective-permute-done.16 = f32[1,16,16,256]{3,2,1,0:T(8,128)S(1)} collective-permute-done((f32[1,16,16,256]{3,2,1,0:T(8,128)S(1)}, f32[1,16,16,256]{3,2,1,0:T(8,128)S(1)}, u32[]{:S(2)}, u32[]{:S(2)}) %collective-permute-start.16) | collective-permute-done | bytes 262176 | tf_op jit(solution)/shard_map/ppermute | solution.py:23
  269.1 9.5 %all-to-all-done = f32[16,1,65536]{2,1,0:T(1,128)} async-done(((f32[16,1,65536]{2,1,0:T(1,128)}), f32[16,1,65536]{2,1,0:T(1,128)}, u32[]{:S(2)}, u32[]{:S(2)}) %all-to-all-start) | async-done | bytes 4194336 | tf_op jit(solution)/shard_map/all_to_all | solution.py:66
  279.1 13.7 %reduce = f32[16,65536]{1,0:T(8,128)} reduce(f32[16,1,65536]{2,1,0:T(1,128)} %all-to-all-done, f32[]{:T(128)} %broadcast.107), dimensions={1}, to_apply=%all_to_all.13.reduce_sub_computation | reduce | bytes 8388612 | tf_op jit(solution)/shard_map/all_to_all | solution.py:66
  292.8 25.7 %reshape.9 = f32[256,16,16,16]{3,2,1,0:T(8,128)} reshape(f32[16,65536]{1,0:T(8,128)} %reduce) | data formatting | bytes 8388608
  318.5 32.0 %copy.14 = f32[16,16,16,16,16]{2,3,4,1,0:T(8,128)} copy(f32[16,16,16,16,16]{2,1,0,4,3:T(8,128)} %bitcast.29) | data formatting | bytes 8388608 | tf_op jit(solution)/shard_map/all_to_all | solution.py:66
  350.5 23.5 %all_to_all.16 = f32[16,16,256,16]{2,3,1,0:T(8,128)} reshape(f32[16,16,16,16,16]{3,2,4,1,0:T(8,128)} %bitcast.30) | data formatting | bytes 8388608 | tf_op jit(solution)/shard_map/all_to_all | solution.py:66
  374.0 7.3 %constant_dynamic-update-slice_fusion.4 = (f32[18,16,16,256]{3,2,1,0:T(8,128)}, f32[16,16,16,256]{3,2,1,0:T(8,128)S(1)}) fusion(f32[18,16,16,256]{3,2,1,0:T(8,128)} %constant_dynamic-update-slice_fusion.5, f32[16,16,16,256]{3,2,1,0:T(8,128)} %param.7, f32[16,16,256,16]{2,3,1,0:T(8,128)} %all_to_all.16), kind=kLoop, calls=%fused_computation.189 | loop fusion | flops 1048576 | bytes 16777216
  382.0 2.8 fusion.179
  384.8 4.8 %collective-permute-start.18 = (f32[18,16,1,256]{3,2,1,0:T(1,128)S(1)}, f32[18,16,1,256]{3,2,1,0:T(1,128)S(1)}, u32[]{:S(2)}, u32[]{:S(2)}) collective-permute-start(f32[18,16,1,256]{3,2,1,0:T(1,128)S(1)} %get-tuple-element.2), channel_id=1, source_target_pairs={{1,0},{2,1},{3,2},{4,3},{5,4},{6,5},{7,6},{8,7},{9,8},{10,9},{11,1... | collective-permute-start | bytes 884744 | tf_op jit(solution)/shard_map/ppermute | solution.py:25
  391.5 2.3 collective-permute-done.18
  393.9 4.7 %collective-permute-done.19 = f32[18,16,1,256]{3,2,1,0:T(1,128)S(1)} collective-permute-done((f32[18,16,1,256]{3,2,1,0:T(1,128)S(1)}, f32[18,16,1,256]{3,2,1,0:T(1,128)S(1)}, u32[]{:S(2)}, u32[]{:S(2)}) %collective-permute-start.19) | collective-permute-done | bytes 294944 | tf_op jit(solution)/shard_map/ppermute | solution.py:23
  398.6 10.2 %fusion.5 = f32[16,16,16,256]{3,2,1,0:T(8,128)} fusion(f32[16,16,16,256]{3,2,1,0:T(8,128)S(1)} %copy-done.4, f32[16,16,16,256]{3,2,1,0:T(8,128)S(1)} %get-tuple-element.13, f32[1,16,16,256]{3,2,1,0:T(8,128)S(1)} %collective-permute-done.16, f32[1,16,16,256]{3,2,1,0:T(8,128)S(1)} %collective-permute-done.17, ...), kind=kOutput, calls=%fused_computation.8 | convolution fusion | flops 3239051264 | bytes 18678784 | tf_op jit(solution)/shard_map/wrks,ts->wrkt/dot_general | solution.py:73
  (44 shorter events, 26.4 us)
Async XLA Ops:
  0.6 31.5 %copy-start = (f32[256,256]{1,0:T(8,128)S(1)}, f32[256,256]{1,0:T(8,128)}, u32[]{:S(2)}) copy-start(f32[256,256]{1,0:T(8,128)} %param.10) | copy-start | bytes 786436
  1.8 10.7 %collective-permute-start = (f32[1,16,16,256]{3,2,1,0:T(8,128)S(1)}, f32[1,16,16,256]{3,2,1,0:T(8,128)S(1)}, u32[]{:S(2)}, u32[]{:S(2)}) collective-permute-start(f32[1,16,16,256]{3,2,1,0:T(8,128)S(1)} %get-tuple-element.25), channel_id=1, source_target_pairs={{0,16},{16,32},{32,48},{48,64},{64,80},{80,96},{96,112},{1,17},{17... | collective-permute-start | bytes 786440 | tf_op jit(solution)/shard_map/ppermute | solution.py:23
  6.9 13.3 %collective-permute-start.1 = (f32[1,16,16,256]{3,2,1,0:T(8,128)S(1)}, f32[1,16,16,256]{3,2,1,0:T(8,128)S(1)}, u32[]{:S(2)}, u32[]{:S(2)}) collective-permute-start(f32[1,16,16,256]{3,2,1,0:T(8,128)S(1)} %get-tuple-element.24), channel_id=1, source_target_pairs={{16,0},{32,16},{48,32},{64,48},{80,64},{96,80},{112,96},{17,1},{33... | collective-permute-start | bytes 786440 | tf_op jit(solution)/shard_map/ppermute | solution.py:25
  12.4 19.7 %copy-start.3 = (f32[16,16,16,256]{3,2,1,0:T(8,128)S(1)}, f32[16,16,16,256]{3,2,1,0:T(8,128)}, u32[]{:S(2)}) copy-start(f32[16,16,16,256]{3,2,1,0:T(8,128)} %param.6) | copy-start | bytes 12582916
  12.4 19.7 %copy-start.5 = (f32[16,16]{1,0:T(8,128)S(1)}, f32[16,16]{1,0:T(8,128)}, u32[]{:S(2)}) copy-start(f32[16,16]{1,0:T(8,128)} %param.8) | copy-start | bytes 3076
  12.5 19.7 %copy-start.7 = (f32[16,16]{1,0:T(8,128)S(1)}, f32[16,16]{1,0:T(8,128)}, u32[]{:S(2)}) copy-start(f32[16,16]{1,0:T(8,128)} %param.9) | copy-start | bytes 3076
  20.8 6.6 %collective-permute-start.2 = (f32[18,16,1,256]{3,2,1,0:T(1,128)S(1)}, f32[18,16,1,256]{3,2,1,0:T(1,128)S(1)}, u32[]{:S(2)}, u32[]{:S(2)}) collective-permute-start(f32[18,16,1,256]{3,2,1,0:T(1,128)S(1)} %get-tuple-element.10), channel_id=1, source_target_pairs={{1,0},{2,1},{3,2},{4,3},{5,4},{6,5},{7,6},{8,7},{9,8},{10,9},{11,1... | collective-permute-start | bytes 884744 | tf_op jit(solution)/shard_map/ppermute | solution.py:25
  23.2 9.0 %collective-permute-start.3 = (f32[18,16,1,256]{3,2,1,0:T(1,128)S(1)}, f32[18,16,1,256]{3,2,1,0:T(1,128)S(1)}, u32[]{:S(2)}, u32[]{:S(2)}) collective-permute-start(f32[18,16,1,256]{3,2,1,0:T(1,128)S(1)} %get-tuple-element.11), channel_id=1, source_target_pairs={{0,1},{1,2},{2,3},{3,4},{4,5},{5,6},{6,7},{7,8},{8,9},{9,10},{10,1... | collective-permute-start | bytes 884744 | tf_op jit(solution)/shard_map/ppermute | solution.py:23
  40.0 8.7 %collective-permute-start.4 = (f32[1,16,16,256]{3,2,1,0:T(8,128)S(1)}, f32[1,16,16,256]{3,2,1,0:T(8,128)S(1)}, u32[]{:S(2)}, u32[]{:S(2)}) collective-permute-start(f32[1,16,16,256]{3,2,1,0:T(8,128)S(1)} %get-tuple-element.23), channel_id=1, source_target_pairs={{0,16},{16,32},{32,48},{48,64},{64,80},{80,96},{96,112},{1,17},{17... | collective-permute-start | bytes 786440 | tf_op jit(solution)/shard_map/ppermute | solution.py:23
  44.9 11.9 %collective-permute-start.5 = (f32[1,16,16,256]{3,2,1,0:T(8,128)S(1)}, f32[1,16,16,256]{3,2,1,0:T(8,128)S(1)}, u32[]{:S(2)}, u32[]{:S(2)}) collective-permute-start(f32[1,16,16,256]{3,2,1,0:T(8,128)S(1)} %get-tuple-element.22), channel_id=1, source_target_pairs={{16,0},{32,16},{48,32},{64,48},{80,64},{96,80},{112,96},{17,1},{33... | collective-permute-start | bytes 786440 | tf_op jit(solution)/shard_map/ppermute | solution.py:25
  57.4 6.1 %collective-permute-start.6 = (f32[18,16,1,256]{3,2,1,0:T(1,128)S(1)}, f32[18,16,1,256]{3,2,1,0:T(1,128)S(1)}, u32[]{:S(2)}, u32[]{:S(2)}) collective-permute-start(f32[18,16,1,256]{3,2,1,0:T(1,128)S(1)} %get-tuple-element.8), channel_id=1, source_target_pairs={{1,0},{2,1},{3,2},{4,3},{5,4},{6,5},{7,6},{8,7},{9,8},{10,9},{11,1... | collective-permute-start | bytes 884744 | tf_op jit(solution)/shard_map/ppermute | solution.py:25
  59.3 8.9 %collective-permute-start.7 = (f32[18,16,1,256]{3,2,1,0:T(1,128)S(1)}, f32[18,16,1,256]{3,2,1,0:T(1,128)S(1)}, u32[]{:S(2)}, u32[]{:S(2)}) collective-permute-start(f32[18,16,1,256]{3,2,1,0:T(1,128)S(1)} %get-tuple-element.9), channel_id=1, source_target_pairs={{0,1},{1,2},{2,3},{3,4},{4,5},{5,6},{6,7},{7,8},{8,9},{9,10},{10,1... | collective-permute-start | bytes 884744 | tf_op jit(solution)/shard_map/ppermute | solution.py:23
  76.4 8.7 %collective-permute-start.8 = (f32[1,16,16,256]{3,2,1,0:T(8,128)S(1)}, f32[1,16,16,256]{3,2,1,0:T(8,128)S(1)}, u32[]{:S(2)}, u32[]{:S(2)}) collective-permute-start(f32[1,16,16,256]{3,2,1,0:T(8,128)S(1)} %get-tuple-element.21), channel_id=1, source_target_pairs={{0,16},{16,32},{32,48},{48,64},{64,80},{80,96},{96,112},{1,17},{17... | collective-permute-start | bytes 786440 | tf_op jit(solution)/shard_map/ppermute | solution.py:23
  81.2 11.3 %collective-permute-start.9 = (f32[1,16,16,256]{3,2,1,0:T(8,128)S(1)}, f32[1,16,16,256]{3,2,1,0:T(8,128)S(1)}, u32[]{:S(2)}, u32[]{:S(2)}) collective-permute-start(f32[1,16,16,256]{3,2,1,0:T(8,128)S(1)} %get-tuple-element.20), channel_id=1, source_target_pairs={{16,0},{32,16},{48,32},{64,48},{80,64},{96,80},{112,96},{17,1},{33... | collective-permute-start | bytes 786440 | tf_op jit(solution)/shard_map/ppermute | solution.py:25
  93.1 6.1 %collective-permute-start.10 = (f32[18,16,1,256]{3,2,1,0:T(1,128)S(1)}, f32[18,16,1,256]{3,2,1,0:T(1,128)S(1)}, u32[]{:S(2)}, u32[]{:S(2)}) collective-permute-start(f32[18,16,1,256]{3,2,1,0:T(1,128)S(1)} %get-tuple-element.6), channel_id=1, source_target_pairs={{1,0},{2,1},{3,2},{4,3},{5,4},{6,5},{7,6},{8,7},{9,8},{10,9},{11,1... | collective-permute-start | bytes 884744 | tf_op jit(solution)/shard_map/ppermute | solution.py:25
  95.0 8.9 %collective-permute-start.11 = (f32[18,16,1,256]{3,2,1,0:T(1,128)S(1)}, f32[18,16,1,256]{3,2,1,0:T(1,128)S(1)}, u32[]{:S(2)}, u32[]{:S(2)}) collective-permute-start(f32[18,16,1,256]{3,2,1,0:T(1,128)S(1)} %get-tuple-element.7), channel_id=1, source_target_pairs={{0,1},{1,2},{2,3},{3,4},{4,5},{5,6},{6,7},{7,8},{8,9},{9,10},{10,1... | collective-permute-start | bytes 884744 | tf_op jit(solution)/shard_map/ppermute | solution.py:23
  112.0 8.5 %collective-permute-start.12 = (f32[1,16,16,256]{3,2,1,0:T(8,128)S(1)}, f32[1,16,16,256]{3,2,1,0:T(8,128)S(1)}, u32[]{:S(2)}, u32[]{:S(2)}) collective-permute-start(f32[1,16,16,256]{3,2,1,0:T(8,128)S(1)} %get-tuple-element.19), channel_id=1, source_target_pairs={{0,16},{16,32},{32,48},{48,64},{64,80},{80,96},{96,112},{1,17},{17... | collective-permute-start | bytes 786440 | tf_op jit(solution)/shard_map/ppermute | solution.py:23
  116.7 11.1 %collective-permute-start.13 = (f32[1,16,16,256]{3,2,1,0:T(8,128)S(1)}, f32[1,16,16,256]{3,2,1,0:T(8,128)S(1)}, u32[]{:S(2)}, u32[]{:S(2)}) collective-permute-start(f32[1,16,16,256]{3,2,1,0:T(8,128)S(1)} %get-tuple-element.18), channel_id=1, source_target_pairs={{16,0},{32,16},{48,32},{64,48},{80,64},{96,80},{112,96},{17,1},{33... | collective-permute-start | bytes 786440 | tf_op jit(solution)/shard_map/ppermute | solution.py:25
  128.4 6.1 %collective-permute-start.14 = (f32[18,16,1,256]{3,2,1,0:T(1,128)S(1)}, f32[18,16,1,256]{3,2,1,0:T(1,128)S(1)}, u32[]{:S(2)}, u32[]{:S(2)}) collective-permute-start(f32[18,16,1,256]{3,2,1,0:T(1,128)S(1)} %get-tuple-element.4), channel_id=1, source_target_pairs={{1,0},{2,1},{3,2},{4,3},{5,4},{6,5},{7,6},{8,7},{9,8},{10,9},{11,1... | collective-permute-start | bytes 884744 | tf_op jit(solution)/shard_map/ppermute | solution.py:25
  130.4 8.9 %collective-permute-start.15 = (f32[18,16,1,256]{3,2,1,0:T(1,128)S(1)}, f32[18,16,1,256]{3,2,1,0:T(1,128)S(1)}, u32[]{:S(2)}, u32[]{:S(2)}) collective-permute-start(f32[18,16,1,256]{3,2,1,0:T(1,128)S(1)} %get-tuple-element.5), channel_id=1, source_target_pairs={{0,1},{1,2},{2,3},{3,4},{4,5},{5,6},{6,7},{7,8},{8,9},{9,10},{10,1... | collective-permute-start | bytes 884744 | tf_op jit(solution)/shard_map/ppermute | solution.py:23
  147.4 11.1 %copy-start.2 = (f32[16,16,16,256]{3,2,1,0:T(8,128)}, f32[16,16,16,256]{3,2,1,0:T(8,128)S(1)}, u32[]{:S(2)}) copy-start(f32[16,16,16,256]{3,2,1,0:T(8,128)S(1)} %fusion.33) | copy-start | bytes 12582916
  147.9 5.8 %collective-permute-start.20 = (f32[16,16,1,256]{3,2,1,0:T(1,128)S(1)}, f32[16,16,1,256]{3,2,1,0:T(1,128)S(1)}, u32[]{:S(2)}, u32[]{:S(2)}) collective-permute-start(f32[16,16,1,256]{3,2,1,0:T(1,128)S(1)} %get-tuple-element.16), channel_id=1, source_target_pairs={{1,0},{2,1},{3,2},{4,3},{5,4},{6,5},{7,6},{8,7},{9,8},{10,9},{11,1... | collective-permute-start | bytes 786440 | tf_op jit(solution)/shard_map/ppermute | solution.py:25
  149.8 8.6 %collective-permute-start.21 = (f32[16,16,1,256]{3,2,1,0:T(1,128)S(1)}, f32[16,16,1,256]{3,2,1,0:T(1,128)S(1)}, u32[]{:S(2)}, u32[]{:S(2)}) collective-permute-start(f32[16,16,1,256]{3,2,1,0:T(1,128)S(1)} %get-tuple-element.17), channel_id=1, source_target_pairs={{0,1},{1,2},{2,3},{3,4},{4,5},{5,6},{6,7},{7,8},{8,9},{9,10},{10,1... | collective-permute-start | bytes 786440 | tf_op jit(solution)/shard_map/ppermute | solution.py:23
  210.0 68.7 %all-to-all-start = ((f32[16,1,65536]{2,1,0:T(1,128)}), f32[16,1,65536]{2,1,0:T(1,128)}, u32[]{:S(2)}, u32[]{:S(2)}) async-start(f32[16,1,65536]{2,1,0:T(1,128)} %reshape.8), calls=%async_computation | async-start | bytes 8388608 | tf_op jit(solution)/shard_map/all_to_all | solution.py:66
  218.2 50.2 %collective-permute-start.16 = (f32[1,16,16,256]{3,2,1,0:T(8,128)S(1)}, f32[1,16,16,256]{3,2,1,0:T(8,128)S(1)}, u32[]{:S(2)}, u32[]{:S(2)}) collective-permute-start(f32[1,16,16,256]{3,2,1,0:T(8,128)S(1)} %get-tuple-element.15), channel_id=1, source_target_pairs={{0,16},{16,32},{32,48},{48,64},{64,80},{80,96},{96,112},{1,17},{17... | collective-permute-start | bytes 786440 | tf_op jit(solution)/shard_map/ppermute | solution.py:23
  222.5 158.8 %collective-permute-start.17 = (f32[1,16,16,256]{3,2,1,0:T(8,128)S(1)}, f32[1,16,16,256]{3,2,1,0:T(8,128)S(1)}, u32[]{:S(2)}, u32[]{:S(2)}) collective-permute-start(f32[1,16,16,256]{3,2,1,0:T(8,128)S(1)} %get-tuple-element.14), channel_id=1, source_target_pairs={{16,0},{32,16},{48,32},{64,48},{80,64},{96,80},{112,96},{17,1},{33... | collective-permute-start | bytes 786440 | tf_op jit(solution)/shard_map/ppermute | solution.py:25
  374.0 24.5 %copy-start.4 = (f32[16,16,16,256]{3,2,1,0:T(8,128)S(1)}, f32[16,16,16,256]{3,2,1,0:T(8,128)}, u32[]{:S(2)}) copy-start(f32[16,16,16,256]{3,2,1,0:T(8,128)} %param.7) | copy-start | bytes 12582916
  374.0 24.5 %copy-start.6 = (f32[256,256]{1,0:T(8,128)S(1)}, f32[256,256]{1,0:T(8,128)}, u32[]{:S(2)}) copy-start(f32[256,256]{1,0:T(8,128)} %param.11) | copy-start | bytes 786436
  384.8 9.0 %collective-permute-start.18 = (f32[18,16,1,256]{3,2,1,0:T(1,128)S(1)}, f32[18,16,1,256]{3,2,1,0:T(1,128)S(1)}, u32[]{:S(2)}, u32[]{:S(2)}) collective-permute-start(f32[18,16,1,256]{3,2,1,0:T(1,128)S(1)} %get-tuple-element.2), channel_id=1, source_target_pairs={{1,0},{2,1},{3,2},{4,3},{5,4},{6,5},{7,6},{8,7},{9,8},{10,9},{11,1... | collective-permute-start | bytes 884744 | tf_op jit(solution)/shard_map/ppermute | solution.py:25
  389.6 8.9 %collective-permute-start.19 = (f32[18,16,1,256]{3,2,1,0:T(1,128)S(1)}, f32[18,16,1,256]{3,2,1,0:T(1,128)S(1)}, u32[]{:S(2)}, u32[]{:S(2)}) collective-permute-start(f32[18,16,1,256]{3,2,1,0:T(1,128)S(1)} %get-tuple-element.3), channel_id=1, source_target_pairs={{0,1},{1,2},{2,3},{3,4},{4,5},{5,6},{6,7},{7,8},{8,9},{9,10},{10,1... | collective-permute-start | bytes 884744 | tf_op jit(solution)/shard_map/ppermute | solution.py:23
  398.6 10.2 %copy-start.1 = (f32[256,256]{1,0:T(8,128)S(1)}, f32[256,256]{1,0:T(8,128)}, u32[]{:S(2)}) copy-start(f32[256,256]{1,0:T(8,128)} %param.10) | copy-start | bytes 786436
where the time goes:
time: 411 us; the launch traced here: 409 us
  local copies, waits for them, and re-layouts  141 us (34%)
  waiting for transfers between devices  133 us (32%)
  starting transfers between devices  65.6 us (16%)
  matrix products  42.1 us (10%)
  other arithmetic  26 us (6%)
    ppermute x11, waiting for transfers between devices, extended(): lax.ppermute(tail, axis, [(i, (i + 1) % count) for i in range(ends)])  84.8 us
    all_to_all x3, local copies, waits for them, and re-layouts, on_device(): lax.all_to_all(action, 'state', split_axis=3, concat_axis=2, tiled=True)  55.9 us
    unnamed x21, local copies, waits for them, and re-layouts  51.7 us
    ppermute x11, waiting for transfers between devices, extended(): lax.ppermute(head, axis, [((i + 1) % count, i) for i in range(ends)])  38.6 us
    ppermute x11, starting transfers between devices, extended(): lax.ppermute(tail, axis, [(i, (i + 1) % count) for i in range(ends)])  37.3 us
    dot_general x4, matrix products, on_device(): jnp.einsum('wrsk,tk->wrst', source, tank_inverse, precision=lax.Precision...  31.9 us
    mul x1, local copies, waits for them, and re-layouts, control_law(): action = -control_bound * jnp.tanh(shifted / (control_cost * control_bound))  26.4 us
    ppermute x11, starting transfers between devices, extended(): lax.ppermute(head, axis, [((i + 1) % count, i) for i in range(ends)])  21.2 us
  transfers between devices with their start and end apart: 23, of which 22 were waited for; matrix products, arithmetic and copies ran while one was open for 21% of the time, Pallas kernels for 0%

commit v1 on v0

v1 whole, which is shorter than its diff:
```python
import jax
import jax.numpy as jnp
from jax import lax
from jax.experimental import pallas as pl
from jax.experimental.pallas import tpu as pltpu
from jax.sharding import PartitionSpec as P

ITERS = 4
MESH = pl.DeviceIdType.MESH

step_size = 0.25
tank_spread = 0.3

F32 = jnp.float32
BF16 = jnp.bfloat16


def split(x):
    hi = x.astype(BF16)
    lo = (x - hi.astype(F32)).astype(BF16)
    return hi, lo


def body(
    price_s,
    rate_s,
    tinv_ref,
    sinv_ref,
    v_hbm,
    d_hbm,
    val_hbm,
    dn_hbm,
    u,
    x,
    rt,
    rs,
    pb,
    qb,
    d,
    dks,
    dkr,
    st,
    vo,
    sb,
    rb,
    ld_sem,
    st_sem,
    hs,
    hr,
    dhs,
    dhr,
    as_sem,
    ar_sem,
    own_sem,
):
    wi = lax.axis_index("wind")
    si = lax.axis_index("state")
    nw = 8
    ns = 16

    halves = (pl.ds(0, 128), pl.ds(128, 128))
    loads_v = [
        pltpu.make_async_copy(v_hbm.at[:, :, halves[kh]], st.at[kh], ld_sem.at[kh]) for kh in range(2)
    ]
    load_d = pltpu.make_async_copy(d_hbm, d.at[pl.ds(1, 16)], ld_sem.at[2])
    for load in loads_v:
        load.start()
    load_d.start()

    barrier = pltpu.get_barrier_semaphore()

    @pl.loop(1, ns)
    def _(p):
        pl.semaphore_signal(
            barrier, inc=1, device_id={"wind": wi, "state": (si + p) % ns}, device_id_type=MESH
        )

    @pl.when(wi > 0)
    def _():
        pl.semaphore_signal(barrier, inc=1, device_id={"wind": wi - 1, "state": si}, device_id_type=MESH)

    @pl.when(wi < nw - 1)
    def _():
        pl.semaphore_signal(barrier, inc=1, device_id={"wind": wi + 1, "state": si}, device_id_type=MESH)

    @pl.when(wi == 0)
    def _():
        d[0] = jnp.zeros((256, 256), F32)

        @pl.loop(0, ITERS)
        def _(n):
            for g in range(2):
                u[n, g, 0] = jnp.zeros((18, 8, 256), F32)

    @pl.when(wi == nw - 1)
    def _():
        d[17] = jnp.zeros((256, 256), F32)

        @pl.loop(0, ITERS)
        def _(n):
            for g in range(2):
                u[n, g, 17] = jnp.zeros((18, 8, 256), F32)

    @pl.when(si == 0)
    def _():
        dkr[0] = jnp.zeros((16, 16, 256), F32)

        @pl.loop(0, ITERS + 1)
        def _(n):
            for g in range(2):
                u[n, g, pl.ds(1, 16), 0] = jnp.zeros((16, 8, 256), F32)

    @pl.when(si == ns - 1)
    def _():
        dkr[1] = jnp.zeros((16, 16, 256), F32)

        @pl.loop(0, ITERS + 1)
        def _(n):
            for g in range(2):
                u[n, g, pl.ds(1, 16), 17] = jnp.zeros((16, 8, 256), F32)

    row = lax.broadcasted_iota(jnp.int32, (8, 128), 0)

    @pl.loop(0, 16)
    def _(w):
        for g in range(2):
            p = jnp.zeros((8, 128), F32)
            q = jnp.zeros((8, 128), F32)
            for r in range(8):
                p = jnp.where(row == r, price_s[w, g * 8 + r], p)
                q = jnp.where(row == r, rate_s[w, g * 8 + r], q)
            pb[g, w] = 0.5 * p
            qb[g, w] = step_size * q

    for inv_ref, out in ((tinv_ref, rt), (sinv_ref, rs)):
        hi, lo = split(inv_ref[...].T)
        out[pl.ds(0, 256)] = hi
        out[pl.ds(256, 256)] = lo

    expected = ns - 1 + jnp.where(wi > 0, 1, 0) + jnp.where(wi < nw - 1, 1, 0)
    pl.semaphore_wait(barrier, expected)

    def wind_copies(n, g):
        down = pltpu.make_async_remote_copy(
            src_ref=u.at[n, g, 1, pl.ds(1, 16)],
            dst_ref=u.at[n, g, 17, pl.ds(1, 16)],
            send_sem=hs.at[n, g, 0],
            recv_sem=hr.at[n, g, 0],
            device_id={"wind": wi - 1, "state": si},
            device_id_type=MESH,
        )
        up = pltpu.make_async_remote_copy(
            src_ref=u.at[n, g, 16, pl.ds(1, 16)],
            dst_ref=u.at[n, g, 0, pl.ds(1, 16)],
            send_sem=hs.at[n, g, 1],
            recv_sem=hr.at[n, g, 1],
            device_id={"wind": wi + 1, "state": si},
            device_id_type=MESH,
        )
        return down, up

    def state_copies(n, g):
        down = pltpu.make_async_remote_copy(
            src_ref=u.at[n, g, pl.ds(1, 16), 1],
            dst_ref=u.at[n, g, pl.ds(1, 16), 17],
            send_sem=hs.at[n, g, 2],
            recv_sem=hr.at[n, g, 2],
            device_id={"wind": wi, "state": si - 1},
            device_id_type=MESH,
        )
        up = pltpu.make_async_remote_copy(
            src_ref=u.at[n, g, pl.ds(1, 16), 16],
            dst_ref=u.at[n, g, pl.ds(1, 16), 0],
            send_sem=hs.at[n, g, 3],
            recv_sem=hr.at[n, g, 3],
            device_id={"wind": wi, "state": si + 1},
            device_id_type=MESH,
        )
        return down, up

    def dens_wind_copies():
        down = pltpu.make_async_remote_copy(
            src_ref=d_hbm.at[0],
            dst_ref=d.at[17],
            send_sem=dhs.at[0],
            recv_sem=dhr.at[0],
            device_id={"wind": wi - 1, "state": si},
            device_id_type=MESH,
        )
        up = pltpu.make_async_remote_copy(
            src_ref=d_hbm.at[15],
            dst_ref=d.at[0],
            send_sem=dhs.at[1],
            recv_sem=dhr.at[1],
            device_id={"wind": wi + 1, "state": si},
            device_id_type=MESH,
        )
        return down, up

    def dens_state_copies():
        down = pltpu.make_async_remote_copy(
            src_ref=dks.at[0],
            dst_ref=dkr.at[1],
            send_sem=dhs.at[2],
            recv_sem=dhr.at[2],
            device_id={"wind": wi, "state": si - 1},
            device_id_type=MESH,
        )
        up = pltpu.make_async_remote_copy(
            src_ref=dks.at[1],
            dst_ref=dkr.at[0],
            send_sem=dhs.at[3],
            recv_sem=dhr.at[3],
            device_id={"wind": wi, "state": si + 1},
            device_id_type=MESH,
        )
        return down, up

    def start(pair, index, last):
        @pl.when(index > 0)
        def _():
            pair[0].start()

        @pl.when(index < last)
        def _():
            pair[1].start()

    def arrive(pair, index, last):
        @pl.when(index < last)
        def _():
            pair[0].wait_recv()

        @pl.when(index > 0)
        def _():
            pair[1].wait_recv()

    def drain(pair, index, last):
        @pl.when(index > 0)
        def _():
            pair[0].wait_send()

        @pl.when(index < last)
        def _():
            pair[1].wait_send()

    start(dens_wind_copies(), wi, nw - 1)

    for load in loads_v:
        load.wait()
    for g in range(2):

        @pl.loop(0, 16)
        def _(w):
            for s in range(16):
                for kh in range(2):
                    u[0, g, w + 1, s + 1, :, halves[kh]] = st[kh, w, pl.ds(g * 128 + s, 8, stride=16), :]

        start(wind_copies(0, g), wi, nw - 1)
        start(state_copies(0, g), si, ns - 1)

    load_d.wait()

    @pl.loop(0, 16)
    def _(w):
        for r in range(16):
            dks[0, w, pl.ds(r, 1), :] = d[w + 1, pl.ds(r * 16, 1), :]
            dks[1, w, pl.ds(r, 1), :] = d[w + 1, pl.ds(r * 16 + 15, 1), :]

    def matmul(r):
        return (
            jnp.dot(x[:, pl.ds(0, 256)], r[pl.ds(0, 256)], preferred_element_type=F32)
            + jnp.dot(x[:, pl.ds(256, 256)], r[pl.ds(0, 256)], preferred_element_type=F32)
            + jnp.dot(x[:, pl.ds(0, 256)], r[pl.ds(256, 256)], preferred_element_type=F32)
        )

    def both(tile):
        return jnp.concatenate([tile, tile], axis=1)[None]

    @pl.loop(0, 2 * ITERS)
    def _(m):
        n = m // 2
        g = m % 2
        arrive(wind_copies(n, g), wi, nw - 1)
        arrive(state_copies(n, g), si, ns - 1)

        @pl.loop(0, 4)
        def _(c):
            @pl.loop(0, 4)
            def _(j):
                w = c * 4 + j
                half = 0.25 * (u[n, g, w + 1, pl.ds(2, 16)] - u[n, g, w + 1, pl.ds(0, 16)]) + both(pb[g, w])
                t = jnp.tanh(half)
                mid = u[n, g, w + 1, pl.ds(1, 16)]
                couple = u[n, g, w + 2, pl.ds(1, 16)] + u[n, g, w, pl.ds(1, 16)] - 2.0 * mid
                source = (
                    u[0, g, w + 1, pl.ds(1, 16)] + 0.5 * t * (t - 2.0 * half) + both(qb[g, w]) * couple
                )
                hi, lo = split(source.reshape(128, 256))
                rows = pl.ds(pl.multiple_of(j * 128, 128), 128)
                x[rows, pl.ds(0, 256)] = hi
                x[rows, pl.ds(256, 256)] = lo

            u[n + 1, g, pl.ds(c * 4 + 1, 4), pl.ds(1, 16)] = matmul(rt).reshape(4, 16, 8, 256)

        @pl.when(n < ITERS - 1)
        def _():
            start(wind_copies(n + 1, g), wi, nw - 1)

        start(state_copies(n + 1, g), si, ns - 1)

        @pl.when(m == 1)
        def _():
            start(dens_state_copies(), si, ns - 1)

    group = lax.broadcasted_iota(jnp.int32, (8, 128), 1) // 16

    def own_copy(g, h):
        return pltpu.make_async_copy(sb.at[g, h, si], rb.at[g, h, si], own_sem.at[g, h])

    @pl.loop(0, 4)
    def _(m):
        g = m // 2
        h = m % 2

        @pl.when(h == 0)
        def _():
            arrive(state_copies(ITERS, g), si, ns - 1)

        @pl.loop(0, 16)
        def _(s):
            for kh in range(2):
                lanes = pl.ds(kh * 128, 128)
                a = []
                for w in range(8):
                    slot = h * 8 + w
                    half = (
                        0.25 * (u[ITERS, g, slot + 1, s + 2, :, lanes] - u[ITERS, g, slot + 1, s, :, lanes])
                        + pb[g, slot]
                    )
                    a.append(-2.0 * jnp.tanh(half))
                for bit in (4, 2, 1):
                    high = (group // bit) % 2 == 1
                    b = [None] * 8
                    for w in range(8):
                        if w & bit == 0:
                            b[w] = jnp.where(high, pltpu.roll(a[w + bit], 16 * bit, 1), a[w])
                            b[w + bit] = jnp.where(high, a[w + bit], pltpu.roll(a[w], 128 - 16 * bit, 1))
                    a = b
                for w in range(8):
                    sb[g, h, kh * 8 + w, pl.ds(pl.multiple_of(s * 8, 8), 8), :] = a[w]

        own_copy(g, h).start()

        @pl.loop(1, ns)
        def _(p):
            to = (si + p) % ns
            pltpu.make_async_remote_copy(
                src_ref=sb.at[g, h, to],
                dst_ref=rb.at[g, h, si],
                send_sem=as_sem.at[g, h],
                recv_sem=ar_sem.at[g, h],
                device_id={"wind": wi, "state": to},
                device_id_type=MESH,
            ).start()

    @pl.loop(0, 16)
    def _(w):
        for g in range(2):
            for s in range(16):
                for kh in range(2):
                    vo[kh, w, pl.ds(g * 128 + s, 8, stride=16), :] = u[ITERS, g, w + 1, s + 1, :, halves[kh]]

    stores_v = [
        pltpu.make_async_copy(vo.at[kh], val_hbm.at[:, :, halves[kh]], st_sem.at[4, kh]) for kh in range(2)
    ]
    for store in stores_v:
        store.start()

    arrive(dens_wind_copies(), wi, nw - 1)
    arrive(dens_state_copies(), si, ns - 1)
    level = lax.broadcasted_iota(jnp.int32, (16, 256), 0)

    @pl.loop(0, 16)
    def _(w):
        @pl.loop(0, 16)
        def _(r):
            rows = pl.ds(pl.multiple_of(r * 16, 16), 16)
            mid = d[w + 1, rows, :]
            above = jnp.where(level == 15, dkr[1, w, pl.ds(r, 1), :], pltpu.roll(mid, 15, 0))
            below = jnp.where(level == 0, dkr[0, w, pl.ds(r, 1), :], pltpu.roll(mid, 1, 0))
            couple = d[w + 2, rows, :] + d[w, rows, :] - 2.0 * mid
            source = (
                mid
                + (step_size * tank_spread) * (above + below - 2.0 * mid)
                + (step_size * rate_s[w, r]) * couple
            )
            for kh in range(2):
                st[kh, w, rows, :] = source[:, kh * 128 : (kh + 1) * 128]

    point = lax.broadcasted_iota(jnp.int32, (128, 256), 1)

    def stores_d(g, h):
        rooms = pl.ds(pl.multiple_of(g * 128, 128), 128)
        return [
            pltpu.make_async_copy(
                st.at[kh, pl.ds(h * 8, 8), rooms],
                dn_hbm.at[pl.ds(h * 8, 8), rooms, halves[kh]],
                st_sem.at[g * 2 + h, kh],
            )
            for kh in range(2)
        ]

    def all_blocks(ref, g, h, sem):
        blocks = ref.at[g, h, pl.ds(0, ns - 1)]
        return pltpu.make_async_copy(blocks, blocks, sem.at[g, h])

    @pl.loop(0, 4)
    def _(m):
        g = m // 2
        h = m % 2
        own_copy(g, h).wait()
        all_blocks(rb, g, h, ar_sem).wait()

        @pl.loop(0, 2)
        def _(c):
            @pl.loop(0, 4)
            def _(j):
                r = c * 4 + j
                rows = pl.ds(pl.multiple_of((g * 8 + r) * 16, 16), 16)
                blocks = [rb[g, h, i, pl.ds(r, 16, stride=8), :] for i in range(ns)]
                drift = jnp.concatenate(blocks, axis=0).T
                flux = drift * d[pl.ds(1 + h * 8, 8), rows, :].reshape(128, 256)
                upper = jnp.where(point == 255, 0.0, pltpu.roll(flux, 255, 1))
                lower = jnp.where(point == 0, 0.0, pltpu.roll(flux, 1, 1))
                still = jnp.concatenate(
                    [st[kh, pl.ds(h * 8, 8), rows, :].reshape(128, 128) for kh in range(2)], axis=1
                )
                source = still - (0.5 * step_size) * (upper - lower)
                hi, lo = split(source)
                at = pl.ds(pl.multiple_of(j * 128, 128), 128)
                x[at, pl.ds(0, 256)] = hi
                x[at, pl.ds(256, 256)] = lo

            out = matmul(rs)
            for j in range(4):
                rows = pl.ds(pl.multiple_of((g * 8 + c * 4 + j) * 16, 16), 16)
                for kh in range(2):
                    st[kh, pl.ds(h * 8, 8), rows, :] = out[
                        j * 128 : (j + 1) * 128, kh * 128 : (kh + 1) * 128
                    ].reshape(8, 16, 128)

        for store in stores_d(g, h):
            store.start()

    @pl.loop(0, 4)
    def _(m):
        g = m // 2
        h = m % 2
        all_blocks(sb, g, h, as_sem).wait()
        for store in stores_d(g, h):
            store.wait()

    @pl.loop(0, 2 * ITERS)
    def _(m):
        n = m // 2
        g = m % 2
        drain(wind_copies(n, g), wi, nw - 1)

    @pl.loop(0, 2 * (ITERS + 1))
    def _(m):
        n = m // 2
        g = m % 2
        drain(state_copies(n, g), si, ns - 1)

    drain(dens_wind_copies(), wi, nw - 1)
    drain(dens_state_copies(), si, ns - 1)
    for store in stores_v:
        store.wait()


def on_device(value_next, density, price, wind_rate, tank_inverse, soc_inverse):
    flat = (16, 256, 256)
    smem = pl.BlockSpec(memory_space=pltpu.SMEM)
    vmem = pl.BlockSpec(memory_space=pltpu.VMEM)
    hbm = pl.BlockSpec(memory_space=pl.ANY)
    dma = pltpu.SemaphoreType.DMA
    value, dens = pl.pallas_call(
        body,
        name="storage_step",
        out_shape=(jax.ShapeDtypeStruct(flat, F32), jax.ShapeDtypeStruct(flat, F32)),
        in_specs=[smem, smem, vmem, vmem, hbm, hbm],
        out_specs=(hbm, hbm),
        scratch_shapes=[
            pltpu.VMEM((ITERS + 1, 2, 18, 18, 8, 256), F32),
            pltpu.VMEM((512, 512), BF16),
            pltpu.VMEM((512, 256), BF16),
            pltpu.VMEM((512, 256), BF16),
            pltpu.VMEM((2, 16, 8, 128), F32),
            pltpu.VMEM((2, 16, 8, 128), F32),
            pltpu.VMEM((18, 256, 256), F32),
            pltpu.VMEM((2, 16, 16, 256), F32),
            pltpu.VMEM((2, 16, 16, 256), F32),
            pltpu.VMEM((2, 16, 256, 128), F32),
            pltpu.VMEM((2, 16, 256, 128), F32),
            pltpu.VMEM((2, 2, 16, 128, 128), F32),
            pltpu.VMEM((2, 2, 16, 128, 128), F32),
            dma((3,)),
            dma((5, 2)),
            dma((ITERS + 1, 2, 4)),
            dma((ITERS + 1, 2, 4)),
            dma((4,)),
            dma((4,)),
            dma((2, 2)),
            dma((2, 2)),
            dma((2, 2)),
        ],
        compiler_params=pltpu.CompilerParams(
            collective_id=0, has_side_effects=True, vmem_limit_bytes=62 * 1024 * 1024
        ),
    )(price, wind_rate, tank_inverse, soc_inverse, value_next.reshape(flat), density.reshape(flat))
    return value.reshape(value_next.shape), dens.reshape(density.shape)


def solution(mesh):
    placed = (
        P("wind", None, "state", None),
        P("wind", None, "state", None),
        P("wind", None),
        P("wind", None),
        P(),
        P(),
    )
    return jax.shard_map(
        on_device,
        mesh=mesh,
        in_specs=placed,
        out_specs=(P("wind", None, "state", None), P("wind", None, "state", None)),
        check_vma=False,
    )
```

time: 411 us -> 161 us (0.39)
  the two profiles are of different devices: /device:TPU:6 before, /device:TPU:73 now
where the time goes in v1:
time: 161 us; the launch traced here: 160 us
  Pallas kernels  153 us (95%)
  local copies, waits for them, and re-layouts  6.97 us (4%)
    pallas_call x1, Pallas kernels, on_device(): pl.pallas_call(body, name='storage_step', out_shape=(jax.ShapeDtypeStruct...  153 us
    unnamed x4, local copies, waits for them, and re-layouts  6.97 us

profile of v1, /device:TPU:73, one launch (start us, length us, event | category | flops | bytes accessed | tf_op | source)
XLA Modules:
  0.0 160.5 jit_solution(14233964136040842037)
XLA Ops:
  0.6 152.9 %storage_step.1 = (f32[16,256,256]{2,1,0:T(8,128)}, f32[16,256,256]{2,1,0:T(8,128)}) custom-call(f32[16,16]{1,0:T(8,128)} %price_s.1, f32[16,16]{1,0:T(8,128)} %rate_s.1, f32[256,256]{1,0:T(8,128)} %tinv_ref.1, f32[256,256]{1,0:T(8,128)} %sinv_ref.1, f32[16,256,256]{2,1,0:T(8,128)} %bitcast.4, f32[16,256,256]{2,1,0:T(8,128)} %bitcast.5), custom_call_target="tpu_custom_call" | custom-call | tf_op jit(solution)/shard_map/storage_step/pallas_call | solution.py:487
  153.5 0.0 copy-start
  153.5 5.0 %copy.10 = f32[16,16,16,256]{3,2,1,0:T(8,128)} copy(f32[16,16,16,256]{3,2,1,0:T(8,128)} %bitcast.7) | data formatting | bytes 8388608
  158.5 0.0 copy-done
  158.5 2.0 %copy.11 = f32[16,16,16,256]{3,2,1,0:T(8,128)} copy(f32[16,16,16,256]{3,2,1,0:T(8,128)S(1)} %bitcast.6) | data formatting | bytes 8388608
Async XLA Ops:
  153.5 5.0 %copy-start = (f32[16,256,256]{2,1,0:T(8,128)S(1)}, f32[16,256,256]{2,1,0:T(8,128)}, u32[]{:S(2)}) copy-start(f32[16,256,256]{2,1,0:T(8,128)} %get-tuple-element.5) | copy-start | bytes 12582916

commit v2 on v1

v2 whole, which is shorter than its diff:
```python
import jax
import jax.numpy as jnp
from jax import lax
from jax.experimental import pallas as pl
from jax.experimental.pallas import tpu as pltpu
from jax.sharding import PartitionSpec as P

ITERS = 4
MESH = pl.DeviceIdType.MESH

step_size = 0.25
tank_spread = 0.3

F32 = jnp.float32
BF16 = jnp.bfloat16


def split(x):
    hi = x.astype(BF16)
    lo = (x - hi.astype(F32)).astype(BF16)
    return hi, lo


def body(
    price_hbm,
    rate_hbm,
    tinv_hbm,
    sinv_hbm,
    v_hbm,
    d_hbm,
    vo,
    do,
    u,
    uf,
    x,
    rt,
    rs,
    pb,
    qb,
    d,
    dks,
    dkr,
    pc,
    sb,
    rb,
    price_s,
    rate_s,
    inv,
    ld_sem,
    hs,
    hr,
    dhs,
    dhr,
    as_sem,
    ar_sem,
    own_sem,
):
    wi = lax.axis_index("wind")
    si = lax.axis_index("state")
    nw = 8
    ns = 16

    halves = (pl.ds(0, 128), pl.ds(128, 128))
    load_v = pltpu.make_async_copy(v_hbm, vo, ld_sem.at[0])
    load_d = pltpu.make_async_copy(d_hbm, d.at[pl.ds(1, 16)], ld_sem.at[1])
    load_v.start()
    load_d.start()
    small = [
        pltpu.make_async_copy(src, dst, ld_sem.at[2 + i])
        for i, (src, dst) in enumerate(
            ((price_hbm, price_s), (rate_hbm, rate_s), (tinv_hbm, inv.at[0]), (sinv_hbm, inv.at[1]))
        )
    ]
    for load in small:
        load.start()

    barrier = pltpu.get_barrier_semaphore()

    @pl.loop(1, ns)
    def _(p):
        pl.semaphore_signal(
            barrier, inc=1, device_id={"wind": wi, "state": (si + p) % ns}, device_id_type=MESH
        )

    @pl.when(wi > 0)
    def _():
        pl.semaphore_signal(barrier, inc=1, device_id={"wind": wi - 1, "state": si}, device_id_type=MESH)

    @pl.when(wi < nw - 1)
    def _():
        pl.semaphore_signal(barrier, inc=1, device_id={"wind": wi + 1, "state": si}, device_id_type=MESH)

    @pl.when(wi == 0)
    def _():
        d[0] = jnp.zeros((256, 256), F32)

        @pl.loop(0, ITERS)
        def _(n):
            for g in range(2):
                u[n, g, 0] = jnp.zeros((18, 8, 256), F32)

    @pl.when(wi == nw - 1)
    def _():
        d[17] = jnp.zeros((256, 256), F32)

        @pl.loop(0, ITERS)
        def _(n):
            for g in range(2):
                u[n, g, 17] = jnp.zeros((18, 8, 256), F32)

    @pl.when(si == 0)
    def _():
        dkr[0] = jnp.zeros((16, 16, 256), F32)

        @pl.loop(0, ITERS)
        def _(n):
            for g in range(2):
                u[n, g, pl.ds(1, 16), 0] = jnp.zeros((16, 8, 256), F32)

    @pl.when(si == ns - 1)
    def _():
        dkr[1] = jnp.zeros((16, 16, 256), F32)

        @pl.loop(0, ITERS)
        def _(n):
            for g in range(2):
                u[n, g, pl.ds(1, 16), 17] = jnp.zeros((16, 8, 256), F32)

    expected = ns - 1 + jnp.where(wi > 0, 1, 0) + jnp.where(wi < nw - 1, 1, 0)
    pl.semaphore_wait(barrier, expected)

    def wind_copies(n, g):
        down = pltpu.make_async_remote_copy(
            src_ref=u.at[n, g, 1, pl.ds(1, 16)],
            dst_ref=u.at[n, g, 17, pl.ds(1, 16)],
            send_sem=hs.at[n, g, 0],
            recv_sem=hr.at[n, g, 0],
            device_id={"wind": wi - 1, "state": si},
            device_id_type=MESH,
        )
        up = pltpu.make_async_remote_copy(
            src_ref=u.at[n, g, 16, pl.ds(1, 16)],
            dst_ref=u.at[n, g, 0, pl.ds(1, 16)],
            send_sem=hs.at[n, g, 1],
            recv_sem=hr.at[n, g, 1],
            device_id={"wind": wi + 1, "state": si},
            device_id_type=MESH,
        )
        return down, up

    def state_copies(n, g):
        down = pltpu.make_async_remote_copy(
            src_ref=u.at[n, g, pl.ds(1, 16), 1],
            dst_ref=u.at[n, g, pl.ds(1, 16), 17],
            send_sem=hs.at[n, g, 2],
            recv_sem=hr.at[n, g, 2],
            device_id={"wind": wi, "state": si - 1},
            device_id_type=MESH,
        )
        up = pltpu.make_async_remote_copy(
            src_ref=u.at[n, g, pl.ds(1, 16), 16],
            dst_ref=u.at[n, g, pl.ds(1, 16), 0],
            send_sem=hs.at[n, g, 3],
            recv_sem=hr.at[n, g, 3],
            device_id={"wind": wi, "state": si + 1},
            device_id_type=MESH,
        )
        return down, up

    def dens_wind_copies():
        down = pltpu.make_async_remote_copy(
            src_ref=d_hbm.at[0],
            dst_ref=d.at[17],
            send_sem=dhs.at[0],
            recv_sem=dhr.at[0],
            device_id={"wind": wi - 1, "state": si},
            device_id_type=MESH,
        )
        up = pltpu.make_async_remote_copy(
            src_ref=d_hbm.at[15],
            dst_ref=d.at[0],
            send_sem=dhs.at[1],
            recv_sem=dhr.at[1],
            device_id={"wind": wi + 1, "state": si},
            device_id_type=MESH,
        )
        return down, up

    def dens_state_copies():
        down = pltpu.make_async_remote_copy(
            src_ref=dks.at[0],
            dst_ref=dkr.at[1],
            send_sem=dhs.at[2],
            recv_sem=dhr.at[2],
            device_id={"wind": wi, "state": si - 1},
            device_id_type=MESH,
        )
        up = pltpu.make_async_remote_copy(
            src_ref=dks.at[1],
            dst_ref=dkr.at[0],
            send_sem=dhs.at[3],
            recv_sem=dhr.at[3],
            device_id={"wind": wi, "state": si + 1},
            device_id_type=MESH,
        )
        return down, up

    def start(pair, index, last):
        @pl.when(index > 0)
        def _():
            pair[0].start()

        @pl.when(index < last)
        def _():
            pair[1].start()

    def arrive(pair, index, last):
        @pl.when(index < last)
        def _():
            pair[0].wait_recv()

        @pl.when(index > 0)
        def _():
            pair[1].wait_recv()

    def drain(pair, index, last):
        @pl.when(index > 0)
        def _():
            pair[0].wait_send()

        @pl.when(index < last)
        def _():
            pair[1].wait_send()

    start(dens_wind_copies(), wi, nw - 1)

    def tile_rows(g, s, kh):
        return pl.ds(g * 256 + (s // 8) * 16 + kh * 8 + s % 8, 8, stride=32)

    load_v.wait()
    for g in range(2):

        @pl.loop(0, 16)
        def _(w):
            for s in range(16):
                for kh in range(2):
                    u[0, g, w + 1, s + 1, :, halves[kh]] = vo[w, tile_rows(g, s, kh), :]

        start(wind_copies(0, g), wi, nw - 1)
        start(state_copies(0, g), si, ns - 1)

    load_d.wait()

    @pl.loop(0, 16)
    def _(w):
        for r in range(16):
            dks[0, w, pl.ds(r, 1), :] = d[w + 1, pl.ds(r * 16, 1), :]
            dks[1, w, pl.ds(r, 1), :] = d[w + 1, pl.ds(r * 16 + 15, 1), :]

    for load in small:
        load.wait()
    row = lax.broadcasted_iota(jnp.int32, (8, 128), 0)

    @pl.loop(0, 16)
    def _(w):
        for g in range(2):
            p = jnp.zeros((8, 128), F32)
            q = jnp.zeros((8, 128), F32)
            for r in range(8):
                p = jnp.where(row == r, price_s[w, g * 8 + r], p)
                q = jnp.where(row == r, rate_s[w, g * 8 + r], q)
            pb[g, w] = 0.5 * p
            qb[g, w] = step_size * q

    group = lax.broadcasted_iota(jnp.int32, (8, 128), 1) // 16
    for g in range(2):
        for h in range(2):
            rb[g, h, pl.ds(0, 8), :] = jnp.zeros((8, 128), F32)
            rb[g, h, pl.ds(2056, 8), :] = jnp.zeros((8, 128), F32)

            @pl.loop(0, 8)
            def _(r):
                p = jnp.zeros((1, 128), F32)
                for w in range(8):
                    p = jnp.where(group[:1] == w, 0.5 * price_s[h * 8 + w, g * 8 + r], p)
                pc[g, h, pl.ds(r, 1), :] = p

    for i, out in enumerate((rt, rs)):
        hi, lo = split(inv[i].T)
        out[pl.ds(0, 256)] = hi
        out[pl.ds(256, 256)] = lo

    def matmul(r):
        return (
            jnp.dot(x[:, pl.ds(0, 256)], r[pl.ds(0, 256)], preferred_element_type=F32)
            + jnp.dot(x[:, pl.ds(256, 256)], r[pl.ds(0, 256)], preferred_element_type=F32)
            + jnp.dot(x[:, pl.ds(0, 256)], r[pl.ds(256, 256)], preferred_element_type=F32)
        )

    def both(tile):
        return jnp.concatenate([tile, tile], axis=1)[None]

    def own_copy(g, h):
        return pltpu.make_async_copy(
            sb.at[g, h, si], rb.at[g, h, pl.ds(pl.multiple_of(8 + si * 128, 8), 128)], own_sem.at[g, h]
        )

    def regroup(g, h):
        @pl.loop(0, 4)
        def _(quad):
            for i in range(4):
                s = quad * 4 + i
                for kh in range(2):
                    a = [uf[g, h * 8 + w, s, :, halves[kh]] for w in range(8)]
                    for bit in (4, 2, 1):
                        high = (group // bit) % 2 == 1
                        b = [None] * 8
                        for w in range(8):
                            if w & bit == 0:
                                b[w] = jnp.where(high, pltpu.roll(a[w + bit], 16 * bit, 1), a[w])
                                b[w + bit] = jnp.where(high, a[w + bit], pltpu.roll(a[w], 128 - 16 * bit, 1))
                        a = b
                    for w in range(8):
                        sb[g, h, kh * 8 + w, pl.ds(pl.multiple_of(s * 8, 8), 8), :] = a[w]

    def send(g, h):
        own_copy(g, h).start()

        @pl.loop(1, ns)
        def _(p):
            to = (si + p) % ns
            pltpu.make_async_remote_copy(
                src_ref=sb.at[g, h, to],
                dst_ref=rb.at[g, h, pl.ds(pl.multiple_of(8 + si * 128, 8), 128)],
                send_sem=as_sem.at[g, h],
                recv_sem=ar_sem.at[g, h],
                device_id={"wind": wi, "state": to},
                device_id_type=MESH,
            ).start()

    @pl.loop(0, 2 * ITERS)
    def _(m):
        n = m // 2
        g = m % 2
        arrive(wind_copies(n, g), wi, nw - 1)
        arrive(state_copies(n, g), si, ns - 1)
        @pl.when(m == 2 * ITERS - 1)
        def _():
            for h in range(2):
                send(0, h)


        @pl.loop(0, 4)
        def _(c):
            @pl.loop(0, 4)
            def _(j):
                w = c * 4 + j
                half = 0.25 * (u[n, g, w + 1, pl.ds(2, 16)] - u[n, g, w + 1, pl.ds(0, 16)]) + both(pb[g, w])
                t = jnp.tanh(half)
                mid = u[n, g, w + 1, pl.ds(1, 16)]
                couple = u[n, g, w + 2, pl.ds(1, 16)] + u[n, g, w, pl.ds(1, 16)] - 2.0 * mid
                source = (
                    u[0, g, w + 1, pl.ds(1, 16)] + 0.5 * t * (t - 2.0 * half) + both(qb[g, w]) * couple
                )
                hi, lo = split(source.reshape(128, 256))
                rows = pl.ds(pl.multiple_of(j * 128, 128), 128)
                x[rows, pl.ds(0, 256)] = hi
                x[rows, pl.ds(256, 256)] = lo

            swept = matmul(rt).reshape(4, 16, 8, 256)

            @pl.when(n < ITERS - 1)
            def _():
                u[n + 1, g, pl.ds(c * 4 + 1, 4), pl.ds(1, 16)] = swept

            @pl.when(n == ITERS - 1)
            def _():
                uf[g, pl.ds(c * 4, 4)] = swept

        @pl.when(n < ITERS - 1)
        def _():
            start(wind_copies(n + 1, g), wi, nw - 1)
            start(state_copies(n + 1, g), si, ns - 1)

        @pl.when(m == 1)
        def _():
            start(dens_state_copies(), si, ns - 1)

        @pl.when(n == ITERS - 1)
        def _():
            for h in range(2):
                regroup(g, h)

            @pl.when(g == 1)
            def _():
                for h in range(2):
                    send(1, h)

    @pl.loop(0, 16)
    def _(w):
        for g in range(2):
            for s in range(16):
                for kh in range(2):
                    vo[w, tile_rows(g, s, kh), :] = uf[g, w, s, :, halves[kh]]

    arrive(dens_wind_copies(), wi, nw - 1)
    arrive(dens_state_copies(), si, ns - 1)
    level = lax.broadcasted_iota(jnp.int32, (16, 256), 0)

    @pl.loop(0, 16)
    def _(w):
        @pl.loop(0, 16)
        def _(r):
            rows = pl.ds(pl.multiple_of(r * 16, 16), 16)
            mid = d[w + 1, rows, :]
            above = jnp.where(level == 15, dkr[1, w, pl.ds(r, 1), :], pltpu.roll(mid, 15, 0))
            below = jnp.where(level == 0, dkr[0, w, pl.ds(r, 1), :], pltpu.roll(mid, 1, 0))
            couple = d[w + 2, rows, :] + d[w, rows, :] - 2.0 * mid
            source = (
                mid
                + (step_size * tank_spread) * (above + below - 2.0 * mid)
                + (step_size * rate_s[w, r]) * couple
            )
            for kh in range(2):
                do[w, pl.ds(r * 2, 2), kh] = source[:, kh * 128 : (kh + 1) * 128].reshape(2, 8, 128)

    point = lax.broadcasted_iota(jnp.int32, (128, 256), 1)

    def all_blocks(g, h, sem):
        blocks = sb.at[g, h, pl.ds(0, ns - 1)]
        return pltpu.make_async_copy(blocks, blocks, sem.at[g, h])

    @pl.loop(0, 4)
    def _(m):
        g = m // 2
        h = m % 2
        own_copy(g, h).wait()
        all_blocks(g, h, ar_sem).wait()

        @pl.loop(0, 2)
        def _(c):
            @pl.loop(0, 4)
            def _(j):
                r = c * 4 + j
                rows = pl.ds(pl.multiple_of((g * 8 + r) * 16, 16), 16)
                tiles = pl.ds((g * 8 + r) * 2, 2)
                above = rb[g, h, pl.ds(r + 16, 256, stride=8), :]
                below = rb[g, h, pl.ds(r, 256, stride=8), :]
                drift = (-2.0 * jnp.tanh(0.25 * (above - below) + pc[g, h, pl.ds(r, 1), :])).T
                flux = drift * d[pl.ds(1 + h * 8, 8), rows, :].reshape(128, 256)
                upper = jnp.where(point == 255, 0.0, pltpu.roll(flux, 255, 1))
                lower = jnp.where(point == 0, 0.0, pltpu.roll(flux, 1, 1))
                still = jnp.concatenate(
                    [do[pl.ds(h * 8, 8), tiles, kh].reshape(128, 128) for kh in range(2)], axis=1
                )
                source = still - (0.5 * step_size) * (upper - lower)
                hi, lo = split(source)
                at = pl.ds(pl.multiple_of(j * 128, 128), 128)
                x[at, pl.ds(0, 256)] = hi
                x[at, pl.ds(256, 256)] = lo

            out = matmul(rs)
            for j in range(4):
                tiles = pl.ds((g * 8 + c * 4 + j) * 2, 2)
                for kh in range(2):
                    do[pl.ds(h * 8, 8), tiles, kh] = out[
                        j * 128 : (j + 1) * 128, kh * 128 : (kh + 1) * 128
                    ].reshape(8, 2, 8, 128)

    @pl.loop(0, 4)
    def _(m):
        g = m // 2
        h = m % 2
        all_blocks(g, h, as_sem).wait()

    @pl.loop(0, 2 * ITERS)
    def _(m):
        n = m // 2
        g = m % 2
        drain(wind_copies(n, g), wi, nw - 1)
        drain(state_copies(n, g), si, ns - 1)

    drain(dens_wind_copies(), wi, nw - 1)
    drain(dens_state_copies(), si, ns - 1)


def on_device(value_next, density, price, wind_rate, tank_inverse, soc_inverse):
    vmem = pl.BlockSpec(memory_space=pltpu.VMEM)
    hbm = pl.BlockSpec(memory_space=pltpu.HBM)
    dma = pltpu.SemaphoreType.DMA
    tiles = value_next.reshape(16, 32, 8, 2, 128).transpose(0, 1, 3, 2, 4).reshape(16, 512, 128)
    value, dens = pl.pallas_call(
        body,
        name="storage_step",
        out_shape=(
            jax.ShapeDtypeStruct((16, 512, 128), F32),
            jax.ShapeDtypeStruct((16, 32, 2, 8, 128), F32),
        ),
        in_specs=[hbm] * 6,
        out_specs=(vmem, vmem),
        scratch_shapes=[
            pltpu.VMEM((ITERS, 2, 18, 18, 8, 256), F32),
            pltpu.VMEM((2, 16, 16, 8, 256), F32),
            pltpu.VMEM((512, 512), BF16),
            pltpu.VMEM((512, 256), BF16),
            pltpu.VMEM((512, 256), BF16),
            pltpu.VMEM((2, 16, 8, 128), F32),
            pltpu.VMEM((2, 16, 8, 128), F32),
            pltpu.VMEM((18, 256, 256), F32),
            pltpu.VMEM((2, 16, 16, 256), F32),
            pltpu.VMEM((2, 16, 16, 256), F32),
            pltpu.VMEM((2, 2, 8, 128), F32),
            pltpu.VMEM((2, 2, 16, 128, 128), F32),
            pltpu.VMEM((2, 2, 2064, 128), F32),
            pltpu.SMEM((16, 16), F32),
            pltpu.SMEM((16, 16), F32),
            pltpu.VMEM((2, 256, 256), F32),
            dma((6,)),
            dma((ITERS, 2, 4)),
            dma((ITERS, 2, 4)),
            dma((4,)),
            dma((4,)),
            dma((2, 2)),
            dma((2, 2)),
            dma((2, 2)),
        ],
        compiler_params=pltpu.CompilerParams(
            collective_id=0, has_side_effects=True, vmem_limit_bytes=42 * 1024 * 1024
        ),
    )(*[pltpu.with_memory_space_constraint(a, pltpu.HBM) for a in (price, wind_rate, tank_inverse, soc_inverse, tiles, density.reshape(16, 256, 256))])

    def whole(out):
        return out.reshape(16, 32, 2, 8, 128).transpose(0, 1, 3, 2, 4).reshape(16, 16, 16, 256)

    return whole(value), whole(dens)


def solution(mesh):
    placed = (
        P("wind", None, "state", None),
        P("wind", None, "state", None),
        P("wind", None),
        P("wind", None),
        P(),
        P(),
    )
    return jax.shard_map(
        on_device,
        mesh=mesh,
        in_specs=placed,
        out_specs=(P("wind", None, "state", None), P("wind", None, "state", None)),
        check_vma=False,
    )
```

time: 161 us -> 154 us (0.957)
  the two profiles are of different devices: /device:TPU:73 before, /device:TPU:25 now
where the time goes in v2:
time: 154 us
  Pallas kernels  149 us (97%)
  local copies, waits for them, and re-layouts  4.03 us (3%)
    pallas_call x1, Pallas kernels, on_device(): pl.pallas_call(body, name='storage_step', out_shape=(jax.ShapeDtypeStruct...  149 us
    unnamed x2, local copies, waits for them, and re-layouts  4.03 us

profile of v2, /device:TPU:25, one launch (start us, length us, event | category | flops | bytes accessed | tf_op | source)
XLA Modules:
  0.0 153.5 jit_solution(12635604448469500368)
XLA Ops:
  0.6 148.8 %storage_step.1 = (f32[16,512,128]{2,1,0:T(8,128)S(1)}, f32[16,32,2,8,128]{4,3,2,1,0:T(8,128)S(1)}) custom-call(f32[16,16]{1,0:T(8,128)} %price_hbm.1, f32[16,16]{1,0:T(8,128)} %rate_hbm.1, f32[256,256]{1,0:T(8,128)} %tinv_hbm.1, f32[256,256]{1,0:T(8,128)} %sinv_hbm.1, f32[16,512,128]{2,1,0:T(8,128)} %bitcast.16, f32[16,256,256]{2,1,0:T(8,128)} %bitcast.17), custom_call_target="tpu_custom_call" | custom-call | tf_op jit(solution)/shard_map/storage_step/pallas_call | solution.py:492
  149.5 2.0 %copy.10 = f32[16,16,16,256]{3,2,1,0:T(8,128)} copy(f32[16,16,16,256]{3,2,1,0:T(8,128)S(1)} %bitcast.15) | data formatting | bytes 8388608
  151.5 2.0 %copy.11 = f32[16,16,16,256]{3,2,1,0:T(8,128)} copy(f32[16,16,16,256]{3,2,1,0:T(8,128)S(1)} %bitcast.14) | data formatting | bytes 8388608

commit v3 on v2

--- a/solution.py
+++ b/solution.py
@@ -46,14 +46,22 @@
     price_s,
     rate_s,
     inv,
+    held,
+    held_d,
     ld_sem,
     hs,
     hr,
+    ss,
+    sr,
     dhs,
     dhr,
+    dss,
+    dsr,
     as_sem,
     ar_sem,
     own_sem,
+    rl,
+    fs,
 ):
     wi = lax.axis_index("wind")
     si = lax.axis_index("state")
@@ -126,62 +134,170 @@
             for g in range(2):
                 u[n, g, pl.ds(1, 16), 17] = jnp.zeros((16, 8, 256), F32)
 
-    expected = ns - 1 + jnp.where(wi > 0, 1, 0) + jnp.where(wi < nw - 1, 1, 0)
+    @pl.when(wi >= 2)
+    def _():
+        pl.semaphore_signal(barrier, inc=1, device_id={"wind": wi - 2, "state": si}, device_id_type=MESH)
+
+    @pl.when(wi < nw - 2)
+    def _():
+        pl.semaphore_signal(barrier, inc=1, device_id={"wind": wi + 2, "state": si}, device_id_type=MESH)
+
+    expected = ns - 1
+    for near in (wi > 0, wi < nw - 1, wi >= 2, wi < nw - 2):
+        expected = expected + jnp.where(near, 1, 0)
     pl.semaphore_wait(barrier, expected)
 
-    def wind_copies(n, g):
-        down = pltpu.make_async_remote_copy(
-            src_ref=u.at[n, g, 1, pl.ds(1, 16)],
-            dst_ref=u.at[n, g, 17, pl.ds(1, 16)],
-            send_sem=hs.at[n, g, 0],
-            recv_sem=hr.at[n, g, 0],
-            device_id={"wind": wi - 1, "state": si},
-            device_id_type=MESH,
-        )
-        up = pltpu.make_async_remote_copy(
-            src_ref=u.at[n, g, 16, pl.ds(1, 16)],
-            dst_ref=u.at[n, g, 0, pl.ds(1, 16)],
-            send_sem=hs.at[n, g, 1],
-            recv_sem=hr.at[n, g, 1],
-            device_id={"wind": wi + 1, "state": si},
-            device_id_type=MESH,
-        )
-        return down, up
+    def wind_part(n, g, up, k):
+        points = pl.ds(1 + 4 * k, 4)
+        return pltpu.make_async_remote_copy(
+            src_ref=u.at[n, g, 16 if up else 1, points],
+            dst_ref=u.at[n, g, 0 if up else 17, points],
+            send_sem=hs.at[n, g, up, k],
+            recv_sem=hr.at[n, g, up, k],
+            device_id={"wind": wi + 1 if up else wi - 1, "state": si},
+            device_id_type=MESH,
+        )
+
+    def wind_relay(n, g, up, k):
+        return pltpu.make_async_remote_copy(
+            src_ref=u.at[n, g, 16 if up else 1, pl.ds(1 + 4 * k, 4)],
+            dst_ref=held.at[2 * n + g, k - 1],
+            send_sem=hs.at[n, g, up, k],
+            recv_sem=rl.at[2 * n + g, k - 1],
+            device_id={"wind": wi + 2 if up else wi - 2, "state": si},
+            device_id_type=MESH,
+        )
+
+    def wind_forward(n, g, up, k):
+        return pltpu.make_async_remote_copy(
+            src_ref=held.at[2 * n + g, k - 1],
+            dst_ref=u.at[n, g, 0 if up else 17, pl.ds(1 + 4 * k, 4)],
+            send_sem=fs.at[2 * n + g, k - 1],
+            recv_sem=hr.at[n, g, up, k],
+            device_id={"wind": wi - 1 if up else wi + 1, "state": si},
+            device_id_type=MESH,
+        )
+
+    def dens_part(up, k):
+        rows = pl.ds(64 * k, 64)
+        return pltpu.make_async_remote_copy(
+            src_ref=d_hbm.at[15 if up else 0, rows],
+            dst_ref=d.at[0 if up else 17, rows],
+            send_sem=dhs.at[up, k],
+            recv_sem=dhr.at[up, k],
+            device_id={"wind": wi + 1 if up else wi - 1, "state": si},
+            device_id_type=MESH,
+        )
+
+    def dens_relay(up, k):
+        return pltpu.make_async_remote_copy(
+            src_ref=d_hbm.at[15 if up else 0, pl.ds(64 * k, 64)],
+            dst_ref=held_d.at[k - 1],
+            send_sem=dhs.at[up, k],
+            recv_sem=rl.at[2 * ITERS, k - 1],
+            device_id={"wind": wi + 2 if up else wi - 2, "state": si},
+            device_id_type=MESH,
+        )
+
+    def dens_forward(up, k):
+        return pltpu.make_async_remote_copy(
+            src_ref=held_d.at[k - 1],
+            dst_ref=d.at[0 if up else 17, pl.ds(64 * k, 64)],
+            send_sem=fs.at[2 * ITERS, k - 1],
+            recv_sem=dhr.at[up, k],
+            device_id={"wind": wi - 1 if up else wi + 1, "state": si},
+            device_id_type=MESH,
+        )
+
+    def both_hold(one, other):
+        return jnp.logical_and(one, other)
+
+    def has(up):
+        return wi < nw - 1 if up else wi > 0
+
+    def by_relay(up, k):
+        if up:
+            return both_hold(wi % 2 == 1, both_hold(wi >= 7 - 2 * k, wi <= 5))
+        return both_hold(wi % 2 == 0, both_hold(wi >= 2, wi <= 2 * k))
+
+    def relays(up, k):
+        if up:
+            return both_hold(wi % 2 == 1, wi >= 9 - 2 * k)
+        return both_hold(wi % 2 == 0, wi <= 2 * k - 2)
+
+    def start_plane(part, relay, up):
+        @pl.when(has(up))
+        def _():
+            part(up, 0).start()
+
+        for k in (1, 2, 3):
+
+            @pl.when(by_relay(up, k))
+            def _():
+                relay(up, k).start()
+
+            @pl.when(both_hold(has(up), jnp.logical_not(by_relay(up, k))))
+            def _():
+                part(up, k).start()
+
+    def start_wind(n, g, up):
+        start_plane(lambda up, k: wind_part(n, g, up, k), lambda up, k: wind_relay(n, g, up, k), up)
+
+    def start_dens(up):
+        start_plane(dens_part, dens_relay, up)
+
+    def arrive_plane(part):
+        for up in (0, 1):
+
+            @pl.when(has(1 - up))
+            def _():
+                for k in range(4):
+                    part(up, k).wait_recv()
+
+    def drain_plane(part, onward):
+        for up in (0, 1):
+
+            @pl.when(has(up))
+            def _():
+                for k in range(4):
+                    part(up, k).wait_send()
+
+            for k in (1, 2, 3):
+
+                @pl.when(relays(up, k))
+                def _():
+                    onward(up, k).wait_send()
+
+    def pass_on(relay, onward):
+        for k in (1, 2, 3):
+            for up in (0, 1):
+
+                @pl.when(relays(up, k))
+                def _():
+                    relay(up, k).wait_recv()
+                    onward(up, k).start()
+
+    def forward(n, g):
+        pass_on(lambda up, k: wind_relay(n, g, up, k), lambda up, k: wind_forward(n, g, up, k))
+
+    def forward_dens():
+        pass_on(dens_relay, dens_forward)
 
     def state_copies(n, g):
         down = pltpu.make_async_remote_copy(
             src_ref=u.at[n, g, pl.ds(1, 16), 1],
             dst_ref=u.at[n, g, pl.ds(1, 16), 17],
-            send_sem=hs.at[n, g, 2],
-            recv_sem=hr.at[n, g, 2],
+            send_sem=ss.at[n, g, 0],
+            recv_sem=sr.at[n, g, 0],
             device_id={"wind": wi, "state": si - 1},
             device_id_type=MESH,
         )
         up = pltpu.make_async_remote_copy(
             src_ref=u.at[n, g, pl.ds(1, 16), 16],
             dst_ref=u.at[n, g, pl.ds(1, 16), 0],
-            send_sem=hs.at[n, g, 3],
-            recv_sem=hr.at[n, g, 3],
+            send_sem=ss.at[n, g, 1],
+            recv_sem=sr.at[n, g, 1],
             device_id={"wind": wi, "state": si + 1},
-            device_id_type=MESH,
-        )
-        return down, up
-
-    def dens_wind_copies():
-        down = pltpu.make_async_remote_copy(
-            src_ref=d_hbm.at[0],
-            dst_ref=d.at[17],
-            send_sem=dhs.at[0],
-            recv_sem=dhr.at[0],
-            device_id={"wind": wi - 1, "state": si},
-            device_id_type=MESH,
-        )
-        up = pltpu.make_async_remote_copy(
-            src_ref=d_hbm.at[15],
-            dst_ref=d.at[0],
-            send_sem=dhs.at[1],
-            recv_sem=dhr.at[1],
-            device_id={"wind": wi + 1, "state": si},
             device_id_type=MESH,
         )
         return down, up
@@ -190,16 +306,16 @@
         down = pltpu.make_async_remote_copy(
             src_ref=dks.at[0],
             dst_ref=dkr.at[1],
-            send_sem=dhs.at[2],
-            recv_sem=dhr.at[2],
+            send_sem=dss.at[0],
+            recv_sem=dsr.at[0],
             device_id={"wind": wi, "state": si - 1},
             device_id_type=MESH,
         )
         up = pltpu.make_async_remote_copy(
             src_ref=dks.at[1],
             dst_ref=dkr.at[0],
-            send_sem=dhs.at[3],
-            recv_sem=dhr.at[3],
+            send_sem=dss.at[1],
+            recv_sem=dsr.at[1],
             device_id={"wind": wi, "state": si + 1},
             device_id_type=MESH,
         )
@@ -232,7 +348,8 @@
         def _():
             pair[1].wait_send()
 
-    start(dens_wind_copies(), wi, nw - 1)
+    start_dens(0)
+    start_dens(1)
 
     def tile_rows(g, s, kh):
         return pl.ds(g * 256 + (s // 8) * 16 + kh * 8 + s % 8, 8, stride=32)
@@ -246,7 +363,8 @@
                 for kh in range(2):
                     u[0, g, w + 1, s + 1, :, halves[kh]] = vo[w, tile_rows(g, s, kh), :]
 
-        start(wind_copies(0, g), wi, nw - 1)
+        start_wind(0, g, 0)
+        start_wind(0, g, 1)
         start(state_copies(0, g), si, ns - 1)
 
     load_d.wait()
@@ -328,7 +446,8 @@
 
         @pl.loop(1, ns)
         def _(p):
-            to = (si + p) % ns
+            q = (3 * p) % ns
+            to = (si // 4 + q // 4) % 4 * 4 + (si // 2 + q // 2) % 2 * 2 + (si + q) % 2
             pltpu.make_async_remote_copy(
                 src_ref=sb.at[g, h, to],
                 dst_ref=rb.at[g, h, pl.ds(pl.multiple_of(8 + si * 128, 8), 128)],
@@ -338,12 +457,23 @@
                 device_id_type=MESH,
             ).start()
 
+    forward(0, 0)
+
     @pl.loop(0, 2 * ITERS)
     def _(m):
         n = m // 2
         g = m % 2
-        arrive(wind_copies(n, g), wi, nw - 1)
+        arrive_plane(lambda up, k: wind_part(n, g, up, k))
         arrive(state_copies(n, g), si, ns - 1)
+
+        @pl.when(m < 2 * ITERS - 1)
+        def _():
+            forward((m + 1) // 2, (m + 1) % 2)
+
+        @pl.when(m == 1)
+        def _():
+            forward_dens()
+
         @pl.when(m == 2 * ITERS - 1)
         def _():
             for h in range(2):
@@ -351,7 +481,9 @@
 
 
         @pl.loop(0, 4)
-        def _(c):
+        def _(turn):
+            c = (turn * 3) % 4
+
             @pl.loop(0, 4)
             def _(j):
                 w = c * 4 + j
@@ -373,13 +505,20 @@
             def _():
                 u[n + 1, g, pl.ds(c * 4 + 1, 4), pl.ds(1, 16)] = swept
 
+                @pl.when(turn == 0)
+                def _():
+                    start_wind(n + 1, g, 0)
+
+                @pl.when(turn == 1)
+                def _():
+                    start_wind(n + 1, g, 1)
+
             @pl.when(n == ITERS - 1)
             def _():
                 uf[g, pl.ds(c * 4, 4)] = swept
 
         @pl.when(n < ITERS - 1)
         def _():
-            start(wind_copies(n + 1, g), wi, nw - 1)
             start(state_copies(n + 1, g), si, ns - 1)
 
         @pl.when(m == 1)
@@ -403,7 +542,7 @@
                 for kh in range(2):
                     vo[w, tile_rows(g, s, kh), :] = uf[g, w, s, :, halves[kh]]
 
-    arrive(dens_wind_copies(), wi, nw - 1)
+    arrive_plane(dens_part)
     arrive(dens_state_copies(), si, ns - 1)
     level = lax.broadcasted_iota(jnp.int32, (16, 256), 0)
 
@@ -439,7 +578,7 @@
 
         @pl.loop(0, 2)
         def _(c):
-            @pl.loop(0, 4)
+            @pl.loop(0, 4, unroll=4)
             def _(j):
                 r = c * 4 + j
                 rows = pl.ds(pl.multiple_of((g * 8 + r) * 16, 16), 16)
@@ -477,10 +616,10 @@
     def _(m):
         n = m // 2
         g = m % 2
-        drain(wind_copies(n, g), wi, nw - 1)
+        drain_plane(lambda up, k: wind_part(n, g, up, k), lambda up, k: wind_forward(n, g, up, k))
         drain(state_copies(n, g), si, ns - 1)
 
-    drain(dens_wind_copies(), wi, nw - 1)
+    drain_plane(dens_part, dens_forward)
     drain(dens_state_copies(), si, ns - 1)
 
 
@@ -515,14 +654,22 @@
             pltpu.SMEM((16, 16), F32),
             pltpu.SMEM((16, 16), F32),
             pltpu.VMEM((2, 256, 256), F32),
+            pltpu.VMEM((2 * ITERS, 3, 4, 8, 256), F32),
+            pltpu.VMEM((3, 64, 256), F32),
             dma((6,)),
-            dma((ITERS, 2, 4)),
-            dma((ITERS, 2, 4)),
-            dma((4,)),
-            dma((4,)),
+            dma((ITERS, 2, 2, 4)),
+            dma((ITERS, 2, 2, 4)),
+            dma((ITERS, 2, 2)),
+            dma((ITERS, 2, 2)),
+            dma((2, 4)),
+            dma((2, 4)),
+            dma((2,)),
+            dma((2,)),
             dma((2, 2)),
             dma((2, 2)),
             dma((2, 2)),
+            dma((2 * ITERS + 1, 3)),
+            dma((2 * ITERS + 1, 3)),
         ],
         compiler_params=pltpu.CompilerParams(
             collective_id=0, has_side_effects=True, vmem_limit_bytes=42 * 1024 * 1024

time: 154 us -> 143 us (0.929)
  the two profiles are of different devices: /device:TPU:25 before, /device:TPU:73 now
where the time goes in v3:
time: 143 us
  Pallas kernels  138 us (97%)
  local copies, waits for them, and re-layouts  4.03 us (3%)
    pallas_call x1, Pallas kernels, on_device(): pl.pallas_call(body, name='storage_step', out_shape=(jax.ShapeDtypeStruct...  138 us
    unnamed x2, local copies, waits for them, and re-layouts  4.03 us

profile of v3, /device:TPU:73, one launch (start us, length us, event | category | flops | bytes accessed | tf_op | source)
XLA Modules:
  0.0 143.1 jit_solution(13321619071148643294)
XLA Ops:
  0.6 138.4 %storage_step.1 = (f32[16,512,128]{2,1,0:T(8,128)S(1)}, f32[16,32,2,8,128]{4,3,2,1,0:T(8,128)S(1)}) custom-call(f32[16,16]{1,0:T(8,128)} %price_hbm.1, f32[16,16]{1,0:T(8,128)} %rate_hbm.1, f32[256,256]{1,0:T(8,128)} %tinv_hbm.1, f32[256,256]{1,0:T(8,128)} %sinv_hbm.1, f32[16,512,128]{2,1,0:T(8,128)} %bitcast.16, f32[16,256,256]{2,1,0:T(8,128)} %bitcast.17), custom_call_target="tpu_custom_call" | custom-call | tf_op jit(solution)/shard_map/storage_step/pallas_call | solution.py:631
  139.1 2.0 %copy.10 = f32[16,16,16,256]{3,2,1,0:T(8,128)} copy(f32[16,16,16,256]{3,2,1,0:T(8,128)S(1)} %bitcast.15) | data formatting | bytes 8388608
  141.1 2.0 %copy.11 = f32[16,16,16,256]{3,2,1,0:T(8,128)} copy(f32[16,16,16,256]{3,2,1,0:T(8,128)S(1)} %bitcast.14) | data formatting | bytes 8388608

commit v4 on v3

--- a/solution.py
+++ b/solution.py
@@ -19,6 +19,47 @@
     hi = x.astype(BF16)
     lo = (x - hi.astype(F32)).astype(BF16)
     return hi, lo
+
+
+def product(x, r):
+    return (
+        jnp.dot(x[:, pl.ds(0, 256)], r[pl.ds(0, 256)], preferred_element_type=F32)
+        + jnp.dot(x[:, pl.ds(256, 256)], r[pl.ds(0, 256)], preferred_element_type=F32)
+        + jnp.dot(x[:, pl.ds(0, 256)], r[pl.ds(256, 256)], preferred_element_type=F32)
+    )
+
+
+def density_part(g, h, x, rs, d, pc, rb, still_ref, out_ref):
+    point = lax.broadcasted_iota(jnp.int32, (128, 256), 1)
+    winds = pl.ds(h * 8, 8)
+
+    @pl.loop(0, 2)
+    def _(c):
+        @pl.loop(0, 4, unroll=4)
+        def _(j):
+            r = c * 4 + j
+            rows = pl.ds(pl.multiple_of((g * 8 + r) * 16, 16), 16)
+            tiles = pl.ds((g * 8 + r) * 2, 2)
+            above = rb[g, h, pl.ds(r + 16, 256, stride=8), :]
+            below = rb[g, h, pl.ds(r, 256, stride=8), :]
+            drift = (-2.0 * jnp.tanh(0.25 * (above - below) + pc[g, h, pl.ds(r, 1), :])).T
+            flux = drift * d[pl.ds(1 + h * 8, 8), rows, :].reshape(128, 256)
+            upper = jnp.where(point == 255, 0.0, pltpu.roll(flux, 255, 1))
+            lower = jnp.where(point == 0, 0.0, pltpu.roll(flux, 1, 1))
+            still = jnp.concatenate(
+                [still_ref[winds, tiles, kh].reshape(128, 128) for kh in range(2)], axis=1
+            )
+            hi, lo = split(still - (0.5 * step_size) * (upper - lower))
+            at = pl.ds(pl.multiple_of(j * 128, 128), 128)
+            x[at, pl.ds(0, 256)] = hi
+            x[at, pl.ds(256, 256)] = lo
+
+        out = product(x, rs)
+        for j in range(4):
+            for kh in range(2):
+                out_ref[:, pl.ds((c * 4 + j) * 2, 2), kh] = out[
+                    j * 128 : (j + 1) * 128, kh * 128 : (kh + 1) * 128
+                ].reshape(8, 2, 8, 128)
 
 
 def body(
@@ -30,19 +71,19 @@
     d_hbm,
     vo,
     do,
+    rs,
+    d,
+    pc,
+    rb,
     u,
     uf,
     x,
     rt,
-    rs,
     pb,
     qb,
-    d,
     dks,
     dkr,
-    pc,
     sb,
-    rb,
     price_s,
     rate_s,
     inv,
@@ -408,13 +449,6 @@
         out[pl.ds(0, 256)] = hi
         out[pl.ds(256, 256)] = lo
 
-    def matmul(r):
-        return (
-            jnp.dot(x[:, pl.ds(0, 256)], r[pl.ds(0, 256)], preferred_element_type=F32)
-            + jnp.dot(x[:, pl.ds(256, 256)], r[pl.ds(0, 256)], preferred_element_type=F32)
-            + jnp.dot(x[:, pl.ds(0, 256)], r[pl.ds(256, 256)], preferred_element_type=F32)
-        )
-
     def both(tile):
         return jnp.concatenate([tile, tile], axis=1)[None]
 
@@ -499,7 +533,7 @@
                 x[rows, pl.ds(0, 256)] = hi
                 x[rows, pl.ds(256, 256)] = lo
 
-            swept = matmul(rt).reshape(4, 16, 8, 256)
+            swept = product(x, rt).reshape(4, 16, 8, 256)
 
             @pl.when(n < ITERS - 1)
             def _():
@@ -563,8 +597,6 @@
             for kh in range(2):
                 do[w, pl.ds(r * 2, 2), kh] = source[:, kh * 128 : (kh + 1) * 128].reshape(2, 8, 128)
 
-    point = lax.broadcasted_iota(jnp.int32, (128, 256), 1)
-
     def all_blocks(g, h, sem):
         blocks = sb.at[g, h, pl.ds(0, ns - 1)]
         return pltpu.make_async_copy(blocks, blocks, sem.at[g, h])
@@ -576,35 +608,9 @@
         own_copy(g, h).wait()
         all_blocks(g, h, ar_sem).wait()
 
-        @pl.loop(0, 2)
-        def _(c):
-            @pl.loop(0, 4, unroll=4)
-            def _(j):
-                r = c * 4 + j
-                rows = pl.ds(pl.multiple_of((g * 8 + r) * 16, 16), 16)
-                tiles = pl.ds((g * 8 + r) * 2, 2)
-                above = rb[g, h, pl.ds(r + 16, 256, stride=8), :]
-                below = rb[g, h, pl.ds(r, 256, stride=8), :]
-                drift = (-2.0 * jnp.tanh(0.25 * (above - below) + pc[g, h, pl.ds(r, 1), :])).T
-                flux = drift * d[pl.ds(1 + h * 8, 8), rows, :].reshape(128, 256)
-                upper = jnp.where(point == 255, 0.0, pltpu.roll(flux, 255, 1))
-                lower = jnp.where(point == 0, 0.0, pltpu.roll(flux, 1, 1))
-                still = jnp.concatenate(
-                    [do[pl.ds(h * 8, 8), tiles, kh].reshape(128, 128) for kh in range(2)], axis=1
-                )
-                source = still - (0.5 * step_size) * (upper - lower)
-                hi, lo = split(source)
-                at = pl.ds(pl.multiple_of(j * 128, 128), 128)
-                x[at, pl.ds(0, 256)] = hi
-                x[at, pl.ds(256, 256)] = lo
-
-            out = matmul(rs)
-            for j in range(4):
-                tiles = pl.ds((g * 8 + c * 4 + j) * 2, 2)
-                for kh in range(2):
-                    do[pl.ds(h * 8, 8), tiles, kh] = out[
-                        j * 128 : (j + 1) * 128, kh * 128 : (kh + 1) * 128
-                    ].reshape(8, 2, 8, 128)
+        @pl.when(m < 3)
+        def _():
+            density_part(g, h, x, rs, d, pc, rb, do, do.at[pl.ds(h * 8, 8), pl.ds(g * 16, 16)])
 
     @pl.loop(0, 4)
     def _(m):
@@ -623,34 +629,55 @@
     drain(dens_state_copies(), si, ns - 1)
 
 
+def finish(value_ref, still_ref, rs, d, pc, rb, value_hbm, dens_hbm, x, last, sem):
+    copies = [
+        pltpu.make_async_copy(value_ref.at[pl.ds(i * 4, 4)], value_hbm.at[pl.ds(i * 4, 4)], sem.at[i])
+        for i in range(4)
+    ]
+    for i, (winds, tiles) in enumerate(
+        ((pl.ds(0, 8), pl.ds(0, 16)), (pl.ds(8, 8), pl.ds(0, 16)), (pl.ds(0, 8), pl.ds(16, 16)))
+    ):
+        copies.append(
+            pltpu.make_async_copy(still_ref.at[winds, tiles], dens_hbm.at[winds, tiles], sem.at[4 + i])
+        )
+    for copy in copies:
+        copy.start()
+    density_part(1, 1, x, rs, d, pc, rb, still_ref, last)
+    ending = pltpu.make_async_copy(last, dens_hbm.at[pl.ds(8, 8), pl.ds(16, 16)], sem.at[7])
+    ending.start()
+    for copy in copies:
+        copy.wait()
+    ending.wait()
+
+
 def on_device(value_next, density, price, wind_rate, tank_inverse, soc_inverse):
     vmem = pl.BlockSpec(memory_space=pltpu.VMEM)
     hbm = pl.BlockSpec(memory_space=pltpu.HBM)
     dma = pltpu.SemaphoreType.DMA
     tiles = value_next.reshape(16, 32, 8, 2, 128).transpose(0, 1, 3, 2, 4).reshape(16, 512, 128)
-    value, dens = pl.pallas_call(
+    value, dens, *rest = pl.pallas_call(
         body,
         name="storage_step",
         out_shape=(
             jax.ShapeDtypeStruct((16, 512, 128), F32),
             jax.ShapeDtypeStruct((16, 32, 2, 8, 128), F32),
+            jax.ShapeDtypeStruct((512, 256), BF16),
+            jax.ShapeDtypeStruct((18, 256, 256), F32),
+            jax.ShapeDtypeStruct((2, 2, 8, 128), F32),
+            jax.ShapeDtypeStruct((2, 2, 2064, 128), F32),
         ),
         in_specs=[hbm] * 6,
-        out_specs=(vmem, vmem),
+        out_specs=(vmem,) * 6,
         scratch_shapes=[
             pltpu.VMEM((ITERS, 2, 18, 18, 8, 256), F32),
             pltpu.VMEM((2, 16, 16, 8, 256), F32),
             pltpu.VMEM((512, 512), BF16),
             pltpu.VMEM((512, 256), BF16),
-            pltpu.VMEM((512, 256), BF16),
             pltpu.VMEM((2, 16, 8, 128), F32),
             pltpu.VMEM((2, 16, 8, 128), F32),
-            pltpu.VMEM((18, 256, 256), F32),
             pltpu.VMEM((2, 16, 16, 256), F32),
             pltpu.VMEM((2, 16, 16, 256), F32),
-            pltpu.VMEM((2, 2, 8, 128), F32),
             pltpu.VMEM((2, 2, 16, 128, 128), F32),
-            pltpu.VMEM((2, 2, 2064, 128), F32),
             pltpu.SMEM((16, 16), F32),
             pltpu.SMEM((16, 16), F32),
             pltpu.VMEM((2, 256, 256), F32),
@@ -672,9 +699,22 @@
             dma((2 * ITERS + 1, 3)),
         ],
         compiler_params=pltpu.CompilerParams(
-            collective_id=0, has_side_effects=True, vmem_limit_bytes=42 * 1024 * 1024
+            collective_id=0, has_side_effects=True, vmem_limit_bytes=33 * 1024 * 1024
         ),
     )(*[pltpu.with_memory_space_constraint(a, pltpu.HBM) for a in (price, wind_rate, tank_inverse, soc_inverse, tiles, density.reshape(16, 256, 256))])
+
+    value, dens = pl.pallas_call(
+        finish,
+        name="finish",
+        out_shape=(
+            jax.ShapeDtypeStruct((16, 512, 128), F32),
+            jax.ShapeDtypeStruct((16, 32, 2, 8, 128), F32),
+        ),
+        in_specs=[vmem] * 6,
+        out_specs=(hbm, hbm),
+        scratch_shapes=[pltpu.VMEM((512, 512), BF16), pltpu.VMEM((8, 16, 2, 8, 128), F32), dma((8,))],
+        compiler_params=pltpu.CompilerParams(vmem_limit_bytes=8 * 1024 * 1024),
+    )(value, dens, *rest)
 
     def whole(out):
         return out.reshape(16, 32, 2, 8, 128).transpose(0, 1, 3, 2, 4).reshape(16, 16, 16, 256)

time: 143 us -> 141 us (0.986)
  local copies, waits for them, and re-layouts: 4.03 us -> 0 us
  Pallas kernels: 138 us -> 140 us
    unnamed x2 -> x0, local copies, waits for them, and re-layouts: 4.03 us -> none
    pallas_call x0 -> x1, Pallas kernels: none -> 3.37 us  [on_device(): pl.pallas_call(finish, name='finish', out_shape=(jax.ShapeDtypeStruct((16...]
    pallas_call x1, Pallas kernels: 138 us -> 137 us  [on_device(): pl.pallas_call(body, name='storage_step', out_shape=(jax.ShapeDtypeStruct...]
where the time goes in v4:
time: 141 us
  Pallas kernels  140 us (99%)
    pallas_call x1, Pallas kernels, on_device(): pl.pallas_call(body, name='storage_step', out_shape=(jax.ShapeDtypeStruct...  137 us
    pallas_call x1, Pallas kernels, on_device(): pl.pallas_call(finish, name='finish', out_shape=(jax.ShapeDtypeStruct((16...  3.37 us

profile of v4, /device:TPU:73, one launch (start us, length us, event | category | flops | bytes accessed | tf_op | source)
XLA Modules:
  0.0 140.7 jit_solution(14038925296260084092)
XLA Ops:
  0.6 136.7 %storage_step.1 = (f32[16,512,128]{2,1,0:T(8,128)S(1)}, f32[16,32,2,8,128]{4,3,2,1,0:T(8,128)S(1)}, bf16[512,256]{1,0:T(8,128)(2,1)S(1)}, f32[18,256,256]{2,1,0:...) custom-call(f32[16,16]{1,0:T(8,128)} %price_hbm.1, f32[16,16]{1,0:T(8,128)} %rate_hbm.1, ...), custom_call_target="tpu_custom_call" | custom-call | tf_op jit(solution)/shard_map/storage_step/pallas_call | solution.py:658
  137.3 3.4 %finish.1 = (f32[16,512,128]{2,1,0:T(8,128)}, f32[16,32,2,8,128]{4,3,2,1,0:T(8,128)}) custom-call(f32[16,512,128]{2,1,0:T(8,128)S(1)} %get-tuple-element.10.value_ref, f32[16,32,2,8,128]{4,3,2,1,0:T(8,128)S(1)} %get-tuple-element.11.still_ref, bf16[512,256]{1,0:T(8,128)(2,1)S(1)} %get-tuple-element.12.rs, f32[18,256,256]{2,1,0:T(8,128)S(1)} %get-tuple-element.13.d, ...), custom_call_target="tpu_custom_call" | custom-call | tf_op jit(solution)/shard_map/finish/pallas_call | solution.py:706

commit v5 on v4

--- a/solution.py
+++ b/solution.py
@@ -555,7 +555,7 @@
         def _():
             start(state_copies(n + 1, g), si, ns - 1)
 
-        @pl.when(m == 1)
+        @pl.when(m == 0)
         def _():
             start(dens_state_copies(), si, ns - 1)
 

time: 141 us -> 141 us (level)
  no operation moved by 1% of the time
where the time goes in v5:
time: 141 us
  Pallas kernels  140 us (99%)
    pallas_call x1, Pallas kernels, on_device(): pl.pallas_call(body, name='storage_step', out_shape=(jax.ShapeDtypeStruct...  137 us
    pallas_call x1, Pallas kernels, on_device(): pl.pallas_call(finish, name='finish', out_shape=(jax.ShapeDtypeStruct((16...  3.37 us

profile of v5, /device:TPU:73, one launch (start us, length us, event | category | flops | bytes accessed | tf_op | source)
XLA Modules:
  0.0 140.8 jit_solution(2794920918615098741)
XLA Ops:
  0.6 136.8 %storage_step.1 = (f32[16,512,128]{2,1,0:T(8,128)S(1)}, f32[16,32,2,8,128]{4,3,2,1,0:T(8,128)S(1)}, bf16[512,256]{1,0:T(8,128)(2,1)S(1)}, f32[18,256,256]{2,1,0:...) custom-call(f32[16,16]{1,0:T(8,128)} %price_hbm.1, f32[16,16]{1,0:T(8,128)} %rate_hbm.1, ...), custom_call_target="tpu_custom_call" | custom-call | tf_op jit(solution)/shard_map/storage_step/pallas_call | solution.py:658
  137.5 3.4 %finish.1 = (f32[16,512,128]{2,1,0:T(8,128)}, f32[16,32,2,8,128]{4,3,2,1,0:T(8,128)}) custom-call(f32[16,512,128]{2,1,0:T(8,128)S(1)} %get-tuple-element.10.value_ref, f32[16,32,2,8,128]{4,3,2,1,0:T(8,128)S(1)} %get-tuple-element.11.still_ref, bf16[512,256]{1,0:T(8,128)(2,1)S(1)} %get-tuple-element.12.rs, f32[18,256,256]{2,1,0:T(8,128)S(1)} %get-tuple-element.13.d, ...), custom_call_target="tpu_custom_call" | custom-call | tf_op jit(solution)/shard_map/finish/pallas_call | solution.py:706
